TPU v7x, 32 devices: a whole 2x2x4 slice. The times are simulated.
32 devices in a mesh: dp: 4 (over x, core), head: 4 (over z), expert: 2 (over y).
Axes of the slice: x: 2, y: 2, z: 4, core: 2. Of those that a mesh axis runs over, the one named last changes fastest.
Arguments:
- tokens: bfloat16 [4, 64, 4096], P('dp', ('head', 'expert')), may hold values from -6 to 6
- cotangent: bfloat16 [4, 64, 4096], P('dp', ('head', 'expert')), may hold values from -1.5 to 1.5
- queries: bfloat16 [4, 64, 32, 128], P('dp', 'expert', 'head'), may hold values from -32 to 32
- key_vectors: bfloat16 [4, 64, 32, 128], P('dp', 'expert', 'head'), may hold values from -32 to 32
- value_routes: int32 [4, 32, 64, 1], P('dp', 'head'), may hold values from 0 to 3; in each aligned block of 8 rows (0 to 7, 8 to 15, ..., all dimensions but the last counted through in order) at most 3 rows name the same one
- output_routes: int32 [4, 32, 64, 1], P('dp', 'head'), may hold values from 0 to 3; in each aligned block of 8 rows (0 to 7, 8 to 15, ..., all dimensions but the last counted through in order) at most 3 rows name the same one
- value_experts: bfloat16 [128, 4096, 128], P(('head', 'expert')), may hold values from -0.09375 to 0.09375
- output_experts: bfloat16 [128, 4096, 128], P(('head', 'expert')), may hold values from -0.09375 to 0.09375
Outputs:
- token_grads: bfloat16 [4, 64, 4096], P('dp', ('head', 'expert'))
- query_grads: bfloat16 [4, 64, 32, 128], P('dp', 'expert', 'head')
- key_grads: bfloat16 [4, 64, 32, 128], P('dp', 'expert', 'head')
- value_grads: bfloat16 [128, 4096, 128], P(('head', 'expert'), 'dp')
- output_grads: bfloat16 [128, 4096, 128], P(('head', 'expert'), 'dp')
Inputs may be any that keep to these rules, and one draw needn't show every extreme that they name: value_routes[b, h, t, 0] is the value expert of head h for token t. In each aligned block of 8 tokens of one sequence and head, no expert is chosen more than 3 times, and in every draw some block has exactly 3 for one expert. output_routes[b, h, t, 0] is the output expert of head h for token t. In each aligned block of 8 tokens of one sequence and head, no expert is chosen more than 3 times, and in every draw some block has exactly 3 for one expert.
All inputs are finite; a program needn't handle non-finite values.
Results may differ from a plain program's by a relative error of at most 0.028.
Values may be sent and summed in bfloat16 or wider, within the bound.
A program may use at most 128 MiB of HBM per device.

v0:
```python
import jax
import jax.numpy as jnp
from jax import lax
from jax.sharding import PartitionSpec as P

E = 4
CAP = 3


def slot_rank(routes):
    onehot = (routes[..., None] == jnp.arange(E, dtype=jnp.int32)).astype(jnp.int32)
    before = jnp.cumsum(onehot, axis=-2) - onehot
    return jnp.sum(before * onehot, axis=-1)


def slot_table(routes):
    rank_of = slot_rank(routes)
    expert_hit = routes[..., None, None, :] == jnp.arange(E, dtype=jnp.int32)[:, None, None]
    place_hit = rank_of[..., None, None, :] == jnp.arange(CAP, dtype=jnp.int32)[:, None]
    return jnp.logical_and(expert_hit, place_hit).astype(jnp.bfloat16)


def local(
    tokens,
    cotangent,
    queries,
    key_vectors,
    value_routes,
    output_routes,
    value_experts,
    output_experts,
):
    head_count = lax.axis_size("head")
    expert_count = lax.axis_size("expert")
    sources = head_count * expert_count
    expert_index = lax.axis_index("expert")
    tok_rows = tokens.shape[1]
    model_width = tokens.shape[2]
    query_rows = queries.shape[1]
    groups = queries.shape[2]
    head_dim = queries.shape[3]
    seq_len = value_routes.shape[2]
    pairs_dev = value_experts.shape[0]
    slot_count = sources * CAP
    score_scale = head_dim ** (-0.5)
    value_local = value_routes[0, :, :, 0]
    output_local = output_routes[0, :, :, 0]

    def own_block(route_part):
        shaped = route_part.reshape(groups, head_count, expert_count, tok_rows)
        return lax.dynamic_index_in_dim(shaped, expert_index, 2, keepdims=False)

    own_pair = jnp.stack([own_block(value_local), own_block(output_local)])
    own_routes = lax.all_to_all(own_pair, "head", split_axis=2, concat_axis=1, tiled=True).reshape(
        2, groups * head_count, tok_rows
    )
    value_table = slot_table(own_routes[0]).reshape(
        head_count, expert_count, pairs_dev, CAP, tok_rows
    )

    def pair_rows(route_part, gathered):
        slot_map = slot_table(route_part.reshape(groups, sources, tok_rows))
        slot_map = jnp.moveaxis(slot_map, 2, 1).reshape(groups * E, sources, CAP, tok_rows)
        slot_map = lax.dynamic_slice_in_dim(slot_map, expert_index * pairs_dev, pairs_dev, 0)
        picked = jnp.einsum(
            "psmt,stw->psmw",
            slot_map,
            gathered.reshape(sources, tok_rows, model_width),
            preferred_element_type=jnp.float32,
        )
        return picked.astype(jnp.bfloat16).reshape(pairs_dev, slot_count, model_width)

    whole_tokens, whole_cotangent = (
        lax.all_gather(tokens[0], ("head", "expert"), axis=0, tiled=True),
        lax.all_gather(cotangent[0], ("head", "expert"), axis=0, tiled=True),
    )
    token_slots = pair_rows(value_local, whole_tokens)
    cotangent_slots = pair_rows(output_local, whole_cotangent)
    value_slots = jnp.einsum(
        "prw,pwk->prk", token_slots, value_experts, preferred_element_type=jnp.float32
    ).astype(jnp.bfloat16)
    upstream_slots = jnp.einsum(
        "prw,pwk->prk", cotangent_slots, output_experts, preferred_element_type=jnp.float32
    ).astype(jnp.bfloat16)
    query_start = expert_index * query_rows
    group_values, group_upstream, all_keys = (
        lax.all_gather(value_slots, "expert", axis=0, tiled=True),
        lax.all_gather(upstream_slots, "expert", axis=0, tiled=True),
        lax.all_gather(key_vectors[0], "expert", axis=0, tiled=True),
    )
    token_source = jnp.arange(seq_len, dtype=jnp.int32) // tok_rows
    head_base = jnp.arange(groups, dtype=jnp.int32)[:, None] * E
    value_rank = slot_rank(value_local.reshape(groups, sources, tok_rows)).reshape(groups, seq_len)
    value_index = (head_base + value_local) * slot_count + token_source * CAP + value_rank
    value_rows = group_values.reshape(-1, head_dim)[value_index]
    output_rank = slot_rank(output_local.reshape(groups, sources, tok_rows)).reshape(
        groups, seq_len
    )
    block_routes = lax.dynamic_slice_in_dim(output_local, query_start, query_rows, 1)
    block_rank = lax.dynamic_slice_in_dim(output_rank, query_start, query_rows, 1)
    block_source = lax.dynamic_slice_in_dim(token_source, query_start, query_rows, 0)
    upstream_index = (head_base + block_routes) * slot_count + block_source * CAP + block_rank
    upstream_rows = group_upstream.reshape(-1, head_dim)[upstream_index]
    query_own = queries[0]
    scores = (
        jnp.einsum("ihc,jhc->hij", query_own, all_keys, preferred_element_type=jnp.float32)
        * score_scale
    )
    query_pos = query_start + jnp.arange(query_rows, dtype=jnp.int32)
    causal = jnp.arange(seq_len, dtype=jnp.int32)[None, :] <= query_pos[:, None]
    row_top = jnp.max(jnp.where(causal, scores, -jnp.inf), axis=-1, keepdims=True)
    weights = jnp.where(causal, jnp.exp(scores - row_top), 0.0)
    probs_full = weights / jnp.sum(weights, axis=-1, keepdims=True)
    prob_half = probs_full.astype(jnp.bfloat16)
    outputs = jnp.einsum(
        "hij,hjc->hic", prob_half, value_rows, preferred_element_type=jnp.float32
    ).astype(jnp.bfloat16)
    row_delta = jnp.sum(outputs.astype(jnp.float32) * upstream_rows.astype(jnp.float32), axis=-1)
    prob_grads = jnp.einsum(
        "hic,hjc->hij", upstream_rows, value_rows, preferred_element_type=jnp.float32
    )
    score_grads = (probs_full * (prob_grads - row_delta[:, :, None])).astype(jnp.bfloat16)
    query_grads = (
        jnp.einsum("hij,jhc->ihc", score_grads, all_keys, preferred_element_type=jnp.float32)
        * score_scale
    ).astype(jnp.bfloat16)
    key_part = (
        jnp.einsum("hij,ihc->jhc", score_grads, query_own, preferred_element_type=jnp.float32)
        * score_scale
    )
    value_part = jnp.einsum(
        "hij,hic->jhc", prob_half, upstream_rows, preferred_element_type=jnp.float32
    )
    key_sum, value_sum = (
        lax.psum_scatter(key_part, "expert", scatter_dimension=0, tiled=True),
        lax.psum_scatter(value_part, "expert", scatter_dimension=0, tiled=True),
    )
    value_half = value_sum.astype(jnp.bfloat16)
    block_value_routes = lax.dynamic_slice_in_dim(value_local, query_start, query_rows, 1).reshape(
        groups, head_count, tok_rows
    )
    value_place = slot_table(block_value_routes)
    output_place = slot_table(block_routes.reshape(groups, head_count, tok_rows))
    value_send = jnp.einsum(
        "hsemt,sthc->hesmc",
        value_place,
        value_half.reshape(head_count, tok_rows, groups, head_dim),
        preferred_element_type=jnp.float32,
    )
    value_send = value_send.astype(jnp.bfloat16).reshape(groups * E, head_count * CAP, head_dim)
    output_send = jnp.einsum(
        "hsemt,hstc->hesmc",
        output_place,
        outputs.reshape(groups, head_count, tok_rows, head_dim),
        preferred_element_type=jnp.float32,
    )
    output_send = output_send.astype(jnp.bfloat16).reshape(groups * E, head_count * CAP, head_dim)
    output_slots, grad_slots = (
        lax.all_to_all(output_send, "expert", split_axis=0, concat_axis=1, tiled=True),
        lax.all_to_all(value_send, "expert", split_axis=0, concat_axis=1, tiled=True),
    )
    value_term = jnp.einsum(
        "prw,prk->pwk", token_slots, grad_slots, preferred_element_type=jnp.float32
    )
    output_term = jnp.einsum(
        "prw,prk->pwk", cotangent_slots, output_slots, preferred_element_type=jnp.float32
    )
    value_grads, output_grads = (
        lax.psum_scatter(
            value_term.astype(jnp.bfloat16), "dp", scatter_dimension=1, tiled=True
        ).astype(jnp.float32),
        lax.psum_scatter(
            output_term.astype(jnp.bfloat16), "dp", scatter_dimension=1, tiled=True
        ).astype(jnp.float32),
    )
    token_terms = jnp.einsum(
        "prk,pwk->prw", grad_slots, value_experts, preferred_element_type=jnp.float32
    ).astype(jnp.bfloat16)
    returned = lax.all_to_all(
        token_terms.reshape(pairs_dev, sources, CAP, model_width),
        ("head", "expert"),
        split_axis=1,
        concat_axis=0,
        tiled=True,
    )
    returned = returned.reshape(head_count, expert_count, pairs_dev, CAP, model_width)
    token_grads = jnp.einsum(
        "gjpmt,gjpmw->tw", value_table, returned, preferred_element_type=jnp.float32
    )
    return (
        token_grads.astype(jnp.bfloat16)[None],
        query_grads[None],
        key_sum.astype(jnp.bfloat16)[None],
        value_grads.astype(jnp.bfloat16),
        output_grads.astype(jnp.bfloat16),
    )


def solution(mesh):
    return jax.shard_map(
        local,
        mesh=mesh,
        in_specs=(
            P("dp", ("head", "expert"), None),
            P("dp", ("head", "expert"), None),
            P("dp", "expert", "head", None),
            P("dp", "expert", "head", None),
            P("dp", "head", None, None),
            P("dp", "head", None, None),
            P(("head", "expert"), None, None),
            P(("head", "expert"), None, None),
        ),
        out_specs=(
            P("dp", ("head", "expert"), None),
            P("dp", "expert", "head", None),
            P("dp", "expert", "head", None),
            P(("head", "expert"), "dp", None),
            P(("head", "expert"), "dp", None),
        ),
        check_vma=False,
    )
```

profile of v0, /device:TPU:0, one launch (start us, length us, event | category | flops | bytes accessed | tf_op | source)
XLA Modules:
  0.0 425.0 jit_solution(12598080767516610200)
XLA Ops:
  8.5 5.1 %reduce_window_sum.48 = s32[8,8,8,4]{2,1,3,0:T(8,128)S(1)} reduce-window(s32[8,8,8,4]{2,1,3,0:T(8,128)S(1)} %fusion.34, s32[]{:T(128)} %constant.62.clone.1), window={size=1x1x8x1 pad=0_0x0_0x7_0x0_0}, to_apply=%region_2.3 | reduce-window | flops 14336 | bytes 16388 | tf_op jit(solution)/shard_map/jit(cumsum)/reduce_window_sum | solution.py:12
  18.5 5.9 %all-gather.1 = bf16[1,64,8,128]{3,1,2,0:T(8,128)(2,1)S(1)} all-gather(bf16[1,32,8,128]{3,1,2,0:T(8,128)(2,1)S(1)} %copy.127), channel_id=3, replica_groups=mesh['dp'=4,'head'=4,'expert'=2] {'expert'}, dimensions={1}, use_global_device_ids=true | all-gather | bytes 196608 | tf_op jit(solution)/shard_map/all_gather | solution.py:89
  24.9 32.5 %all-gather = bf16[1,64,4096]{2,1,0:T(8,128)(2,1)S(1)} all-gather(bf16[1,8,4096]{2,1,0:T(8,128)(2,1)} %param.9), channel_id=2, replica_groups=mesh['dp'=4,'head'=4,'expert'=2] {'head','expert'}, dimensions={1}, use_global_device_ids=true | all-gather | bytes 589824 | tf_op jit(solution)/shard_map/all_gather | solution.py:75
  58.6 8.3 %fusion.10 = bf16[16,24,128]{2,1,0:T(8,128)(2,1)S(1)} fusion(bf16[16,4096,128]{2,1,0:T(8,128)(2,1)} %param.15, bf16[16,24,4096]{2,0,1:T(8,128)(2,1)S(1)} %bitcast.123), kind=kOutput, calls=%fused_computation.20 | convolution fusion | flops 402702336 | bytes 20021248 | tf_op jit(solution)/shard_map/prw,pwk->prk/dot_general | solution.py:82
  66.9 5.3 %all_gather.16 = bf16[32,24,128]{2,1,0:T(8,128)(2,1)S(1)} all-gather(bf16[16,24,128]{2,1,0:T(8,128)(2,1)S(1)} %fusion.10), channel_id=1, replica_groups=mesh['dp'=4,'head'=4,'expert'=2] {'expert'}, dimensions={0}, use_global_device_ids=true | all-gather | bytes 294912 | tf_op jit(solution)/shard_map/all_gather | solution.py:88
  75.3 2.3 convolution_bitcast_fusion.1
  78.3 5.1 %reduce_window_sum.50 = s32[8,8,8,4]{2,1,3,0:T(8,128)S(1)} reduce-window(s32[8,8,8,4]{2,1,3,0:T(8,128)S(1)} %fusion.33, s32[]{:T(128)} %constant.62.clone.1), window={size=1x1x8x1 pad=0_0x0_0x7_0x0_0}, to_apply=%region_9.10 | reduce-window | flops 14336 | bytes 16388 | tf_op jit(solution)/shard_map/jit(cumsum)/reduce_window_sum | solution.py:12
  85.3 2.6 reduce_window_sum.51
  89.6 31.5 %all-gather.2 = bf16[1,64,4096]{2,1,0:T(8,128)(2,1)S(1)} all-gather(bf16[1,8,4096]{2,1,0:T(8,128)(2,1)} %param.8), channel_id=4, replica_groups=mesh['dp'=4,'head'=4,'expert'=2] {'head','expert'}, dimensions={1}, use_global_device_ids=true | all-gather | bytes 589824 | tf_op jit(solution)/shard_map/all_gather | solution.py:74
  122.4 10.1 %fusion.13 = bf16[16,24,128]{2,1,0:T(8,128)(2,1)S(1)} fusion(bf16[16,4096,128]{2,1,0:T(8,128)(2,1)} %param.14, bf16[16,24,4096]{2,0,1:T(8,128)(2,1)S(1)} %bitcast.125), kind=kOutput, calls=%fused_computation.21 | convolution fusion | flops 402702336 | bytes 20021248 | tf_op jit(solution)/shard_map/prw,pwk->prk/dot_general | solution.py:79
  132.5 5.4 %all_gather.19 = bf16[32,24,128]{2,1,0:T(8,128)(2,1)S(1)} all-gather(bf16[16,24,128]{2,1,0:T(8,128)(2,1)S(1)} %fusion.13), channel_id=1, replica_groups=mesh['dp'=4,'head'=4,'expert'=2] {'expert'}, dimensions={0}, use_global_device_ids=true | all-gather | bytes 294912 | tf_op jit(solution)/shard_map/all_gather | solution.py:87
  143.2 3.4 all-to-all-start.3
  149.0 2.0 all-to-all-done.3
  151.0 8.8 %convolution_convert_fusion = bf16[16,4096,128]{2,1,0:T(8,128)(2,1)} fusion(bf16[16,24,4096]{2,0,1:T(8,128)(2,1)S(1)} %bitcast.124, bf16[16,24,128]{2,0,1:T(8,128)(2,1)S(1)} %bitcast.133), kind=kOutput, calls=%fused_computation.3 | convolution fusion | flops 411041792 | bytes 20021248 | tf_op jit(solution)/shard_map/prw,prk->pwk/dot_general | solution.py:165
  160.7 2.6 reduce_window_sum.49
  164.7 6.8 %all_to_all.66 = bf16[32,12,128]{2,1,0:T(8,128)(2,1)S(1)} all-to-all(bf16[32,12,128]{2,1,0:T(8,128)(2,1)S(1)} %copy.132), channel_id=1, replica_groups=mesh['dp'=4,'head'=4,'expert'=2] {'expert'}, dimensions={0} | all-to-all | bytes 196608 | tf_op jit(solution)/shard_map/all_to_all | solution.py:160
  171.6 13.1 %convolution_convert_fusion.1 = bf16[16,4096,128]{2,1,0:T(8,128)(2,1)} fusion(bf16[16,24,4096]{2,0,1:T(8,128)(2,1)S(1)} %bitcast.126, bf16[16,24,128]{2,0,1:T(8,128)(2,1)S(1)} %bitcast.131), kind=kOutput, calls=%fused_computation.4 | convolution fusion | flops 411041792 | bytes 20021248 | tf_op jit(solution)/shard_map/prw,prk->pwk/dot_general | solution.py:162
  187.8 4.1 all-to-all-start
  191.9 15.1 %convolution_convert_fusion.4 = bf16[16,24,4096]{2,1,0:T(8,128)(2,1)S(1)} fusion(bf16[16,4096,128]{2,1,0:T(8,128)(2,1)} %param.14, bf16[16,24,128]{2,0,1:T(8,128)(2,1)S(1)} %bitcast.132), kind=kOutput, calls=%fused_computation.7 | convolution fusion | flops 404226048 | bytes 20021248 | tf_op jit(solution)/shard_map/prk,pwk->prw/dot_general | solution.py:176
  207.0 3.4 copy.136
  210.4 5.3 %all-to-all-start.2 = ((bf16[16,8,3,4096]{3,0,2,1:T(8,128)(2,1)}), bf16[16,8,3,4096]{3,0,2,1:T(8,128)(2,1)S(1)}, u32[]{:S(2)}, u32[]{:S(2)}) async-start(bf16[16,8,3,4096]{3,0,2,1:T(8,128)(2,1)} %bitcast.128), calls=%async_computation.3 | async-start | bytes 6291456 | tf_op jit(solution)/shard_map/all_to_all | solution.py:179
  220.0 47.7 %all-to-all-done.2 = bf16[16,8,3,4096]{3,0,2,1:T(8,128)(2,1)S(1)} async-done(((bf16[16,8,3,4096]{3,0,2,1:T(8,128)(2,1)}), bf16[16,8,3,4096]{3,0,2,1:T(8,128)(2,1)S(1)}, u32[]{:S(2)}, u32[]{:S(2)}) %all-to-all-start.2) | async-done | bytes 3145760 | tf_op jit(solution)/shard_map/all_to_all | solution.py:179
  268.9 21.6 %reduce-scatter.11.cloned.1.call-done = bf16[16,1024,128]{2,1,0:T(8,128)(2,1)} async-done(((bf16[16,4096,128]{2,1,0:T(8,128)(2,1)}), bf16[16,1024,128]{2,1,0:T(8,128)(2,1)}) %reduce-scatter.11.cloned.1.call-update) | async-done | bytes 4194320 | tf_op jit(solution)/shard_map/reduce_scatter | solution.py:172
  290.5 128.0 %reduce-scatter.9.cloned.1.call-done = bf16[16,1024,128]{2,1,0:T(8,128)(2,1)} async-done(((bf16[16,4096,128]{2,1,0:T(8,128)(2,1)}), bf16[16,1024,128]{2,1,0:T(8,128)(2,1)}) %reduce-scatter.9.cloned.1.call-update) | async-done | bytes 4194320 | tf_op jit(solution)/shard_map/reduce_scatter | solution.py:169
  (140 shorter events, 34.9 us)
Async XLA Ops:
  7.2 156.3 %reduce-scatter.5.cloned.1.call-start = ((), (), s32[]{:S(2)}) async-start(), calls=%async_computation.8 | async-start | bytes 393216 | tf_op jit(solution)/shard_map/reduce_scatter | solution.py:136
  7.2 17.6 %copy-start.13 = (s32[8]{0:T(128)}, s32[8]{0:T(128)S(1)}, u32[]{:S(2)}) copy-start(s32[8]{0:T(128)S(1)} %iota_multiply_fusion) | copy-start | bytes 100
  13.8 61.5 %copy-start.10 = (pred[32,64]{1,0:T(8,128)(4,1)}, pred[32,64]{1,0:T(8,128)(4,1)S(1)}, u32[]{:S(2)}) copy-start(pred[32,64]{1,0:T(8,128)(4,1)S(1)} %iota_compare_fusion.11) | copy-start | bytes 6148
  16.8 61.5 %copy-start.3 = (s32[8,8,8]{2,1,0:T(8,128)}, s32[8,8,8]{2,1,0:T(8,128)S(1)}, u32[]{:S(2)}) copy-start(s32[8,8,8]{2,1,0:T(8,128)S(1)} %eq.327) | copy-start | bytes 6148
  58.6 13.6 %copy-start.4 = (bf16[1,32,8,128]{3,2,1,0:T(8,128)(2,1)S(1)}, bf16[1,32,8,128]{3,2,1,0:T(8,128)(2,1)}, u32[]{:S(2)}) copy-start(bf16[1,32,8,128]{3,2,1,0:T(8,128)(2,1)} %param.10) | copy-start | bytes 196612
  72.4 0.7 copy-start.2
  73.8 4.5 %copy-start.11 = (f32[8,32]{1,0:T(8,128)}, f32[8,32]{1,0:T(8,128)S(1)}, u32[]{:S(2)}) copy-start(f32[8,32]{1,0:T(8,128)S(1)} %get-tuple-element.34) | copy-start | bytes 3076
  122.4 10.1 %copy-start = (bf16[8,16,3,4096]{3,1,2,0:T(8,128)(2,1)}, bf16[8,16,3,4096]{3,1,2,0:T(8,128)(2,1)S(1)}, u32[]{:S(2)}) copy-start(bf16[8,16,3,4096]{3,1,2,0:T(8,128)(2,1)S(1)} %convolution_convert_fusion.2) | copy-start | bytes 9437188
  122.4 17.4 %copy-start.12 = (f32[8,32]{1,0:T(8,128)S(1)}, f32[8,32]{1,0:T(8,128)}, u32[]{:S(2)}) copy-start(f32[8,32]{1,0:T(8,128)} %copy-done.11) | copy-start | bytes 3076
  132.5 15.3 %copy-start.5 = (bf16[1,32,8,128]{3,2,1,0:T(8,128)(2,1)S(1)}, bf16[1,32,8,128]{3,2,1,0:T(8,128)(2,1)}, u32[]{:S(2)}) copy-start(bf16[1,32,8,128]{3,2,1,0:T(8,128)(2,1)} %param.10) | copy-start | bytes 196612
  143.2 7.8 %all-to-all-start.3 = ((bf16[32,12,128]{2,1,0:T(8,128)(2,1)}), bf16[32,12,128]{2,1,0:T(8,128)(2,1)S(1)}, u32[]{:S(2)}, u32[]{:S(2)}) async-start(bf16[32,12,128]{2,1,0:T(8,128)(2,1)} %copy.147), calls=%async_computation.6 | async-start | bytes 262144 | tf_op jit(solution)/shard_map/all_to_all | solution.py:159
  146.5 71.8 %reduce-scatter.7.cloned.1.call-start = ((), (), s32[]{:S(2)}) async-start(), calls=%async_computation.9 | async-start | bytes 393216 | tf_op jit(solution)/shard_map/reduce_scatter | solution.py:135
  147.8 12.1 %copy-start.6 = (bf16[8,32,64]{2,1,0:T(8,128)(2,1)}, bf16[8,32,64]{2,1,0:T(8,128)(2,1)S(1)}, u32[]{:S(2)}) copy-start(bf16[8,32,64]{2,1,0:T(8,128)(2,1)S(1)} %fusion.20) | copy-start | bytes 98308
  148.7 141.7 %reduce-scatter.11.cloned.1.call-start = ((), (), s32[]{:S(2)}) async-start(), calls=%async_computation.11 | async-start | bytes 20971520 | tf_op jit(solution)/shard_map/reduce_scatter | solution.py:172
  159.9 0.7 copy-start.8
  159.9 11.7 %copy-start.1 = (bf16[8,16,3,4096]{3,1,2,0:T(8,128)(2,1)S(1)}, bf16[8,16,3,4096]{3,1,2,0:T(8,128)(2,1)}, u32[]{:S(2)}) copy-start(bf16[8,16,3,4096]{3,1,2,0:T(8,128)(2,1)} %copy-done) | copy-start | bytes 9437188
  159.9 258.6 %reduce-scatter.9.cloned.1.call-start = ((), (), s32[]{:S(2)}) async-start(), calls=%async_computation.10 | async-start | bytes 20971520 | tf_op jit(solution)/shard_map/reduce_scatter | solution.py:169
  184.7 0.7 copy-start.9
  187.8 22.6 %all-to-all-start = ((s32[4,1,128]{2,1,0:T(1,128)}), s32[4,1,128]{2,1,0:T(1,128)S(1)}, u32[]{:S(2)}, u32[]{:S(2)}) async-start(s32[4,1,128]{2,1,0:T(1,128)} %reshape.346), calls=%async_computation | async-start | bytes 4096 | tf_op jit(solution)/shard_map/all_to_all | solution.py:54
  210.4 5.4 %copy-start.7 = (bf16[8,32,64]{2,1,0:T(8,128)(2,1)S(1)}, bf16[8,32,64]{2,1,0:T(8,128)(2,1)}, u32[]{:S(2)}) copy-start(bf16[8,32,64]{2,1,0:T(8,128)(2,1)} %copy-done.6) | copy-start | bytes 98308
  210.4 57.2 %all-to-all-start.2 = ((bf16[16,8,3,4096]{3,0,2,1:T(8,128)(2,1)}), bf16[16,8,3,4096]{3,0,2,1:T(8,128)(2,1)S(1)}, u32[]{:S(2)}, u32[]{:S(2)}) async-start(bf16[16,8,3,4096]{3,0,2,1:T(8,128)(2,1)} %bitcast.128), calls=%async_computation.3 | async-start | bytes 6291456 | tf_op jit(solution)/shard_map/all_to_all | solution.py:179
Sparse Core Ops, SparseCore 0:
  77.7 12.9 reduce-scatter.4
  149.6 12.7 reduce-scatter.6
  165.5 124.9 reduce-scatter.10
  293.5 124.9 reduce-scatter.8
where the time goes:
time: 426 us; the launch traced here: 425 us
  waiting for transfers between devices  199 us (47%)
  blocking collectives  87.4 us (21%)
  matrix products  67.6 us (16%)
  other arithmetic  23.7 us (6%)
  local copies, waits for them, and re-layouts  19.6 us (5%)
  between operations  14.3 us (3%)
  starting transfers between devices  13.1 us (3%)
    reduce_scatter x1, waiting for transfers between devices, local(): lax.psum_scatter(value_term.astype(jnp.bfloat16), 'dp', scatter_dimension...  128 us
    all_to_all x1, waiting for transfers between devices, local(): lax.all_to_all(token_terms.reshape(pairs_dev, sources, CAP, model_width),...  47.7 us
    all_gather x1, blocking collectives, local(): lax.all_gather(cotangent[0], ('head', 'expert'), axis=0, tiled=True)  32.5 us
    all_gather x1, blocking collectives, local(): lax.all_gather(tokens[0], ('head', 'expert'), axis=0, tiled=True)  31.5 us
    reduce_scatter x1, waiting for transfers between devices, local(): lax.psum_scatter(output_term.astype(jnp.bfloat16), 'dp', scatter_dimensio...  21.6 us
    another operation x5, other arithmetic, slot_rank(): before = jnp.cumsum(onehot, axis=-2) - onehot  15.4 us
    dot_general x1, matrix products, local(): jnp.einsum('prk,pwk->prw', grad_slots, value_experts, preferred_element_t...  15.1 us
    dot_general x1, matrix products, local(): jnp.einsum('prw,prk->pwk', token_slots, grad_slots, preferred_element_typ...  13.1 us
  transfers between devices with their start and end apart: 7, of which 4 were waited for; matrix products, arithmetic and copies ran while one was open for 20% of the time, Pallas kernels for 0%

commit v1 on v0

--- a/solution.py
+++ b/solution.py
@@ -196,9 +196,142 @@
     )
 
 
+def exchanged(
+    tokens,
+    cotangent,
+    queries,
+    key_vectors,
+    value_routes,
+    output_routes,
+    value_experts,
+    output_experts,
+):
+    dp_count = lax.axis_size("dp")
+    dp_index = lax.axis_index("dp")
+    expert_count = lax.axis_size("expert")
+    expert_index = lax.axis_index("expert")
+    sources = lax.axis_size("head") * expert_count
+    tok_rows = tokens.shape[1]
+    width = tokens.shape[2] // dp_count
+    groups = queries.shape[2]
+    head_dim = queries.shape[3]
+    seq_len = value_routes.shape[2]
+    pairs_dev = value_experts.shape[0]
+    own_heads = groups // expert_count
+    score_scale = head_dim ** (-0.5)
+
+    rows = jnp.stack([tokens[0], cotangent[0]])
+    rows = lax.all_to_all(rows, "dp", split_axis=2, concat_axis=1, tiled=True)
+    rows = lax.all_gather(
+        rows.reshape(2, dp_count, tok_rows, width), ("head", "expert"), axis=2, tiled=True
+    )
+    token_rows = rows[0].reshape(dp_count * seq_len, width)
+    cotangent_rows = rows[1].reshape(dp_count * seq_len, width)
+
+    routes = jnp.stack([value_routes[0, :, :, 0], output_routes[0, :, :, 0]])
+    routes = lax.dynamic_slice_in_dim(routes, expert_index * own_heads, own_heads, 1)
+    routes = lax.all_gather(routes, "dp", axis=1)
+    picks = jnp.moveaxis(routes, 3, 2)[..., None] == jnp.arange(E, dtype=jnp.int32)
+    picks = picks.reshape(2, dp_count * seq_len, own_heads, E, 1)
+
+    pair = jnp.stack([queries[0], key_vectors[0]])
+    pair = lax.all_to_all(pair, "expert", split_axis=2, concat_axis=1, tiled=True)
+    query_all, key_all = pair[0], pair[1]
+
+    value_weight = lax.dynamic_slice_in_dim(value_experts, dp_index * width, width, 1)
+    output_weight = lax.dynamic_slice_in_dim(output_experts, dp_index * width, width, 1)
+
+    def project(source_rows, weight, pick):
+        every = jnp.einsum("td,pdk->tpk", source_rows, weight, preferred_element_type=jnp.float32)
+        every = every.reshape(dp_count * seq_len, own_heads, E, head_dim)
+        return jnp.sum(jnp.where(pick, every, 0.0), axis=2).astype(jnp.bfloat16)
+
+    part = jnp.stack(
+        [
+            project(token_rows, value_weight, picks[0]).reshape(
+                dp_count, seq_len, own_heads, head_dim
+            ),
+            project(cotangent_rows, output_weight, picks[1]).reshape(
+                dp_count, seq_len, own_heads, head_dim
+            ),
+        ],
+        axis=1,
+    )
+    part = lax.all_to_all(part, "dp", split_axis=0, concat_axis=0, tiled=True)
+    whole = jnp.sum(part.astype(jnp.float32), axis=0).astype(jnp.bfloat16)
+    values, upstream = whole[0], whole[1]
+
+    scores = (
+        jnp.einsum("ihc,jhc->hij", query_all, key_all, preferred_element_type=jnp.float32)
+        * score_scale
+    )
+    position = jnp.arange(seq_len, dtype=jnp.int32)
+    causal = position[None, :] <= position[:, None]
+    row_top = jnp.max(jnp.where(causal, scores, -jnp.inf), axis=-1, keepdims=True)
+    weights = jnp.where(causal, jnp.exp(scores - row_top), 0.0)
+    probs = weights / jnp.sum(weights, axis=-1, keepdims=True)
+    prob_half = probs.astype(jnp.bfloat16)
+    outputs = jnp.einsum(
+        "hij,jhc->ihc", prob_half, values, preferred_element_type=jnp.float32
+    ).astype(jnp.bfloat16)
+    row_delta = jnp.sum(outputs.astype(jnp.float32) * upstream.astype(jnp.float32), axis=-1)
+    prob_grads = jnp.einsum("ihc,jhc->hij", upstream, values, preferred_element_type=jnp.float32)
+    value_half = jnp.einsum(
+        "hij,ihc->jhc", prob_half, upstream, preferred_element_type=jnp.float32
+    ).astype(jnp.bfloat16)
+    score_grads = (probs * (prob_grads - row_delta.T[:, :, None])).astype(jnp.bfloat16)
+    query_grads = (
+        jnp.einsum("hij,jhc->ihc", score_grads, key_all, preferred_element_type=jnp.float32)
+        * score_scale
+    ).astype(jnp.bfloat16)
+    key_grads = (
+        jnp.einsum("hij,ihc->jhc", score_grads, query_all, preferred_element_type=jnp.float32)
+        * score_scale
+    ).astype(jnp.bfloat16)
+
+    factors = lax.all_gather(jnp.stack([value_half, outputs]), "dp", axis=1)
+    factors = factors.reshape(2, dp_count * seq_len, own_heads, 1, head_dim)
+    factors = jnp.where(picks, factors, jnp.zeros((), jnp.bfloat16)).reshape(
+        2, dp_count * seq_len, pairs_dev, head_dim
+    )
+    token_part = jnp.einsum(
+        "tpk,pdk->td", factors[0], value_weight, preferred_element_type=jnp.float32
+    ).astype(jnp.bfloat16)
+    token_part = lax.all_to_all(
+        token_part.reshape(dp_count * sources, tok_rows, width),
+        ("dp", "head", "expert"),
+        split_axis=0,
+        concat_axis=0,
+        tiled=True,
+    )
+    token_grads = jnp.sum(
+        token_part.reshape(dp_count, sources, tok_rows, width).astype(jnp.float32), axis=1
+    ).astype(jnp.bfloat16)
+    token_grads = jnp.moveaxis(token_grads, 0, 1).reshape(tok_rows, dp_count * width)
+    value_grads = jnp.einsum(
+        "td,tpk->pdk", token_rows, factors[0], preferred_element_type=jnp.float32
+    ).astype(jnp.bfloat16)
+    output_grads = jnp.einsum(
+        "td,tpk->pdk", cotangent_rows, factors[1], preferred_element_type=jnp.float32
+    ).astype(jnp.bfloat16)
+    back = lax.all_to_all(
+        jnp.stack([query_grads, key_grads]), "expert", split_axis=1, concat_axis=2, tiled=True
+    )
+    return token_grads[None], back[0][None], back[1][None], value_grads, output_grads
+
+
+def chosen(*args):
+    groups, pairs_dev = args[2].shape[2], args[6].shape[0]
+    expert_count = lax.axis_size("expert")
+    whole_heads = groups % expert_count == 0 and pairs_dev == groups // expert_count * E
+    if whole_heads and args[0].shape[2] % (lax.axis_size("dp") * 128) == 0:
+        return exchanged(*args)
+    return local(*args)
+
+
 def solution(mesh):
     return jax.shard_map(
-        local,
+        chosen,
         mesh=mesh,
         in_specs=(
             P("dp", ("head", "expert"), None),

time: 426 us -> 139 us (0.33)
  waiting for transfers between devices: 199 us -> 31.7 us
  blocking collectives: 87.4 us -> 20.5 us
  matrix products: 67.6 us -> 15.7 us
  other arithmetic: 23.7 us -> 5.27 us
  local copies, waits for them, and re-layouts: 19.6 us -> 35.6 us
    reduce_scatter x4 -> x0, waiting for transfers between devices: 150 us -> none  [the longest x1 128 us: local(): lax.psum_scatter(value_term.astype(jnp.bfloat16), 'dp', scatter_dimension...]
    all_gather x5 -> x2, blocking collectives: 80.6 us -> 11.8 us  [the longest x1 6.63 us: exchanged(): factors = lax.all_gather(jnp.stack([value_half, outputs]), 'dp', axis=1)]
    dot_general x16 -> x11, matrix products: 67.6 us -> 15.7 us  [the longest x2 4.89 us: project(): jnp.einsum('td,pdk->tpk', source_rows, weight, preferred_element_type=jnp...]
    all_to_all x3 -> x4, waiting for transfers between devices: 49.7 us -> 8.56 us  [the longest x1 8.55 us: exchanged(): part = lax.all_to_all(part, 'dp', split_axis=0, concat_axis=0, tiled=True)]
    all_gather x0 -> x1, waiting for transfers between devices: none -> 23.2 us  [exchanged(): lax.all_gather(rows.reshape(2, dp_count, tok_rows, width), ('head', 'expe...]
    another operation x5 -> x6, other arithmetic: 15.4 us -> 2.74 us  [the longest x1 1.14 us: exchanged(): jnp.stack([project(token_rows, value_weight, picks[0]).reshape(dp_count,...]
    unnamed x38 -> x20, local copies, waits for them, and re-layouts: 5.98 us -> 17.5 us
    dynamic_slice x7 -> x1, local copies, waits for them, and re-layouts: 1.76 us -> 7.79 us  [exchanged(): lax.dynamic_slice_in_dim(output_experts, dp_index * width, width, 1)]
  transfers between devices with their start and end apart: 7 -> 5, of which waited for: 4 -> 2; matrix products, arithmetic and copies ran while one was open for 20% -> 25% of each run, Pallas kernels for 0% -> 0%
where the time goes in v1:
time: 139 us; the launch traced here: 138 us
  local copies, waits for them, and re-layouts  35.6 us (26%)
  waiting for transfers between devices  31.7 us (23%)
  blocking collectives  20.5 us (15%)
  matrix products  15.7 us (11%)
  starting transfers between devices  14.9 us (11%)
  between operations  14.4 us (10%)
  other arithmetic  5.27 us (4%)
    all_gather x1, waiting for transfers between devices, exchanged(): lax.all_gather(rows.reshape(2, dp_count, tok_rows, width), ('head', 'expe...  23.2 us
    unnamed x20, local copies, waits for them, and re-layouts  17.5 us
    all_to_all x1, blocking collectives, exchanged(): rows = lax.all_to_all(rows, 'dp', split_axis=2, concat_axis=1, tiled=True)  8.64 us
    all_to_all x1, waiting for transfers between devices, exchanged(): part = lax.all_to_all(part, 'dp', split_axis=0, concat_axis=0, tiled=True)  8.55 us
    dynamic_slice x1, local copies, waits for them, and re-layouts, exchanged(): lax.dynamic_slice_in_dim(output_experts, dp_index * width, width, 1)  7.79 us
    all_gather x1, blocking collectives, exchanged(): factors = lax.all_gather(jnp.stack([value_half, outputs]), 'dp', axis=1)  6.63 us
    all_gather x1, blocking collectives, exchanged(): routes = lax.all_gather(routes, 'dp', axis=1)  5.21 us
    dot_general x2, matrix products, project(): jnp.einsum('td,pdk->tpk', source_rows, weight, preferred_element_type=jnp...  4.89 us
  transfers between devices with their start and end apart: 5, of which 2 were waited for; matrix products, arithmetic and copies ran while one was open for 25% of the time, Pallas kernels for 0%

profile of v1, /device:TPU:0, one launch (start us, length us, event | category | flops | bytes accessed | tf_op | source)
XLA Modules:
  0.0 138.1 jit_solution(9172476691813793022)
XLA Ops:
  8.1 2.8 %copy.61 = bf16[2,8,4096]{1,0,2:T(2,128)(2,1)S(1)} copy(bf16[2,8,4096]{2,1,0:T(8,128)(2,1)S(1)} %pad_maximum_fusion.2) | data formatting | bytes 262144 | tf_op jit(solution)/shard_map/stack | solution.py:223
  10.9 2.2 %reshape.83 = bf16[4,2,8192]{2,1,0:T(2,128)(2,1)S(1)} reshape(bf16[4096,2,8]{2,1,0:T(2,128)(2,1)S(1)} %bitcast.116) | data formatting | bytes 262144
  13.2 8.6 %all_to_all.55 = bf16[4,2,8192]{2,1,0:T(2,128)(2,1)S(1)} all-to-all(bf16[4,2,8192]{2,1,0:T(2,128)(2,1)S(1)} %reshape.83), channel_id=1, replica_groups=mesh['dp'=4,'head'=4,'expert'=2] {'dp'}, dimensions={0} | all-to-all | bytes 262144 | tf_op jit(solution)/shard_map/all_to_all | solution.py:224
  21.8 2.4 %reshape.84 = bf16[4096,2,8]{2,1,0:T(2,128)(2,1)S(1)} reshape(bf16[4,2,8192]{2,1,0:T(2,128)(2,1)S(1)} %all_to_all.55) | data formatting | bytes 262144
  24.2 3.2 %copy.62 = bf16[2,8,4,1024]{3,1,2,0:T(8,128)(2,1)} copy(bf16[2,8,4,1024]{1,0,3,2:T(2,128)(2,1)S(1)} %bitcast.117) | data formatting | bytes 262144 | tf_op jit(solution)/shard_map/all_to_all | solution.py:224
  28.2 3.4 %all-to-all-start.2 = ((bf16[2,32,8,128]{3,1,0,2:T(8,128)(2,1)}), bf16[2,32,8,128]{3,1,0,2:T(8,128)(2,1)S(1)}, u32[]{:S(2)}, u32[]{:S(2)}) async-start(bf16[2,32,8,128]{3,1,0,2:T(8,128)(2,1)} %pad_maximum_fusion.1), calls=%async_computation.2 | async-start | bytes 262144 | tf_op jit(solution)/shard_map/all_to_all | solution.py:238
  31.6 5.2 %all-gather = s32[2,16,64]{2,0,1:T(2,128)S(1)} all-gather(s32[2,4,64]{2,0,1:T(2,128)S(1)} %fusion.17), channel_id=2, replica_groups=mesh['dp'=4,'head'=4,'expert'=2] {'dp'}, dimensions={1}, use_global_device_ids=true | all-gather | bytes 10240 | tf_op jit(solution)/shard_map/all_gather | solution.py:233
  37.2 7.8 %constant_dynamic-slice_fusion = (bf16[16,1024,128]{2,1,0:T(8,128)(2,1)}, bf16[16,1024,128]{2,1,0:T(8,128)(2,1)}) fusion(bf16[16,4096,128]{2,1,0:T(8,128)(2,1)} %param.15, s32[]{:T(128)S(6)} %select_n.26, bf16[16,4096,128]{2,1,0:T(8,128)(2,1)} %param.14), kind=kLoop, calls=%fused_computation.48 | loop fusion | bytes 16777220 | tf_op jit(solution)/shard_map/dynamic_slice | solution.py:242
  45.0 23.2 %all-gather.4.cloned.1.call-done = bf16[2,4,64,1024]{3,2,1,0:T(8,128)(2,1)} async-done(((bf16[2,4,8,1024]{3,2,1,0:T(8,128)(2,1)}), bf16[2,4,64,1024]{3,2,1,0:T(8,128)(2,1)}) %all-gather.4.cloned.1.call-update) | async-done | bytes 1048592 | tf_op jit(solution)/shard_map/all_gather | solution.py:225
  68.2 1.3 fusion.30
  69.5 3.3 %select_reduce_fusion = bf16[256,4,128]{2,0,1:T(8,128)(2,1)S(1)} fusion(bf16[256,1024,1,1]{1,0,3,2:T(8,128)(2,1)S(1)} %bitcast.125, bf16[4,4,128,1024]{2,3,1,0:T(8,128)(2,1)} %bitcast.119, pred[256,4,4]{0,2,1:T(4,128)(4,1)S(1)} %broadcast_in_dim.69), kind=kOutput, calls=%fused_computation.3 | convolution fusion | flops 1074659328 | bytes 4984832 | tf_op jit(solution)/shard_map/td,pdk->tpk/dot_general | solution.py:245
  73.2 1.5 %select_reduce_fusion.1 = bf16[256,4,128]{2,0,1:T(8,128)(2,1)S(1)} fusion(bf16[256,1024,1,1]{1,0,3,2:T(8,128)(2,1)S(1)} %bitcast.123, bf16[4,4,128,1024]{2,3,1,0:T(8,128)(2,1)S(1)} %bitcast.118, pred[256,4,4]{0,2,1:T(4,128)(4,1)S(1)} %broadcast_in_dim.66), kind=kOutput, calls=%fused_computation.4 | convolution fusion | flops 1074659328 | bytes 4984832 | tf_op jit(solution)/shard_map/td,pdk->tpk/dot_general | solution.py:245
  75.0 1.1 pad_maximum_fusion
  76.1 3.5 %all-to-all-start.1 = ((bf16[4,2,64,4,128]{4,3,2,1,0:T(4,128)(2,1)}), bf16[4,2,64,4,128]{4,3,2,1,0:T(4,128)(2,1)S(1)}, u32[]{:S(2)}, u32[]{:S(2)}) async-start(bf16[4,2,64,4,128]{4,3,2,1,0:T(4,128)(2,1)} %pad_maximum_fusion), calls=%async_computation.1 | async-start | bytes 1048576 | tf_op jit(solution)/shard_map/all_to_all | solution.py:260
  79.8 8.5 %all-to-all-done.1 = bf16[4,2,64,4,128]{4,3,2,1,0:T(4,128)(2,1)S(1)} async-done(((bf16[4,2,64,4,128]{4,3,2,1,0:T(4,128)(2,1)}), bf16[4,2,64,4,128]{4,3,2,1,0:T(4,128)(2,1)S(1)}, u32[]{:S(2)}, u32[]{:S(2)}) %all-to-all-start.1) | async-done | bytes 524320 | tf_op jit(solution)/shard_map/all_to_all | solution.py:260
  90.6 3.4 %all-to-all-start.4 = ((bf16[2,64,4,128]{3,2,0,1:T(4,128)(2,1)}), bf16[2,64,4,128]{3,2,0,1:T(4,128)(2,1)S(1)}, u32[]{:S(2)}, u32[]{:S(2)}) async-start(bf16[2,64,4,128]{3,2,0,1:T(4,128)(2,1)} %copy.75), calls=%async_computation.4 | async-start | bytes 262144 | tf_op jit(solution)/shard_map/all_to_all | solution.py:317
  94.0 6.6 %all-gather.1 = bf16[2,256,4,128]{3,1,2,0:T(8,128)(2,1)S(1)} all-gather(bf16[2,64,4,128]{3,1,2,0:T(8,128)(2,1)S(1)} %pad_maximum_fusion.3), channel_id=3, replica_groups=mesh['dp'=4,'head'=4,'expert'=2] {'dp'}, dimensions={1}, use_global_device_ids=true | all-gather | bytes 655360 | tf_op jit(solution)/shard_map/all_gather | solution.py:292
  100.6 1.4 %broadcast_select_fusion = bf16[2,256,4,4,128]{4,1,3,2,0:T(8,128)(2,1)S(1)} fusion(pred[2,256,4,4]{1,3,2,0:T(4,128)(4,1)S(1)} %iota_compare_fusion.2, bf16[2,256,4,128]{3,1,2,0:T(8,128)(2,1)S(1)} %all-gather.1), kind=kLoop, calls=%fused_computation.5 | loop fusion | flops 1048576 | bytes 2629632 | tf_op jit(solution)/shard_map/jit(_where)/select_n | solution.py:294
  102.2 2.1 %fusion.2 = bf16[32,8,1024]{2,1,0:T(8,128)(2,1)} fusion(bf16[256,16,128]{2,0,1:T(8,128)(2,1)S(1)} %bitcast.120, bf16[16,1024,128]{2,1,0:T(8,128)(2,1)S(1)} %copy-done.1), kind=kOutput, calls=%fused_computation.8 | convolution fusion | flops 1074003968 | bytes 5767168 | tf_op jit(solution)/shard_map/tpk,pdk->td/dot_general | solution.py:297
  104.3 4.6 %all-to-all-start.3 = ((bf16[32,8,1024]{2,1,0:T(8,128)(2,1)}), bf16[32,8,1024]{2,1,0:T(8,128)(2,1)S(1)}, u32[]{:S(2)}, u32[]{:S(2)}) async-start(bf16[32,8,1024]{2,1,0:T(8,128)(2,1)} %fusion.2), calls=%async_computation.3 | async-start | bytes 1048576 | tf_op jit(solution)/shard_map/all_to_all | solution.py:300
  108.9 4.3 %convert_bitcast_fusion = bf16[16,1024,128]{1,2,0:T(8,128)(2,1)} fusion(bf16[256,16,128]{2,0,1:T(8,128)(2,1)S(1)} %bitcast.122, bf16[256,1024,1]{1,0,2:T(8,128)(2,1)} %bitcast.126), kind=kOutput, calls=%fused_computation.1 | convolution fusion | flops 1075838976 | bytes 5767168 | tf_op jit(solution)/shard_map/td,tpk->pdk/dot_general | solution.py:314
  113.3 6.4 %copy.81 = bf16[16,1024,128]{2,1,0:T(8,128)(2,1)} copy(bf16[16,1024,128]{1,2,0:T(8,128)(2,1)} %convert_bitcast_fusion) | data formatting | bytes 8388608
  119.6 3.2 %convert_bitcast_fusion.1 = bf16[16,1024,128]{1,2,0:T(8,128)(2,1)} fusion(bf16[256,16,128]{2,0,1:T(8,128)(2,1)S(1)} %bitcast.121, bf16[256,1024,1]{1,0,2:T(8,128)(2,1)S(1)} %bitcast.124), kind=kOutput, calls=%fused_computation.2 | convolution fusion | flops 1075838976 | bytes 5767168 | tf_op jit(solution)/shard_map/td,tpk->pdk/dot_general | solution.py:311
  122.9 6.4 %copy.80 = bf16[16,1024,128]{2,1,0:T(8,128)(2,1)} copy(bf16[16,1024,128]{1,2,0:T(8,128)(2,1)} %convert_bitcast_fusion.1) | data formatting | bytes 8388608
  (53 shorter events, 7.1 us)
Async XLA Ops:
  7.2 61.1 %all-gather.4.cloned.1.call-start = ((), (), s32[]{:S(2)}) async-start(), calls=%async_computation.5 | async-start | bytes 1179648 | tf_op jit(solution)/shard_map/all_gather | solution.py:225
  8.1 19.4 %copy-start.3 = (bf16[1,32,8,128]{3,2,1,0:T(8,128)(2,1)S(1)}, bf16[1,32,8,128]{3,2,1,0:T(8,128)(2,1)}, u32[]{:S(2)}) copy-start(bf16[1,32,8,128]{3,2,1,0:T(8,128)(2,1)} %param.10) | copy-start | bytes 196612
  8.1 19.4 %copy-start.4 = (bf16[1,32,8,128]{3,2,1,0:T(8,128)(2,1)S(1)}, bf16[1,32,8,128]{3,2,1,0:T(8,128)(2,1)}, u32[]{:S(2)}) copy-start(bf16[1,32,8,128]{3,2,1,0:T(8,128)(2,1)} %param.11) | copy-start | bytes 196612
  10.9 20.7 %copy-start.5 = (s32[1,8,64,1]{2,3,1,0:T(1,128)S(1)}, s32[1,8,64,1]{2,3,1,0:T(1,128)}, u32[]{:S(2)}) copy-start(s32[1,8,64,1]{2,3,1,0:T(1,128)} %param.12) | copy-start | bytes 6148
  10.9 20.7 %copy-start.6 = (s32[1,8,64,1]{2,3,1,0:T(1,128)S(1)}, s32[1,8,64,1]{2,3,1,0:T(1,128)}, u32[]{:S(2)}) copy-start(s32[1,8,64,1]{2,3,1,0:T(1,128)} %param.13) | copy-start | bytes 6148
  28.2 16.8 %all-to-all-start.2 = ((bf16[2,32,8,128]{3,1,0,2:T(8,128)(2,1)}), bf16[2,32,8,128]{3,1,0,2:T(8,128)(2,1)S(1)}, u32[]{:S(2)}, u32[]{:S(2)}) async-start(bf16[2,32,8,128]{3,1,0,2:T(8,128)(2,1)} %pad_maximum_fusion.1), calls=%async_computation.2 | async-start | bytes 262144 | tf_op jit(solution)/shard_map/all_to_all | solution.py:238
  69.5 5.2 %copy-start.2 = (bf16[1,4,64,1024]{3,2,1,0:T(8,128)(2,1)}, bf16[1,4,64,1024]{3,2,1,0:T(8,128)(2,1)S(1)}, u32[]{:S(2)}) copy-start(bf16[1,4,64,1024]{3,2,1,0:T(8,128)(2,1)S(1)} %get-tuple-element.28) | copy-start | bytes 1572868
  69.5 3.6 %copy-start = (bf16[16,1024,128]{2,1,0:T(8,128)(2,1)S(1)}, bf16[16,1024,128]{2,1,0:T(8,128)(2,1)}, u32[]{:S(2)}) copy-start(bf16[16,1024,128]{2,1,0:T(8,128)(2,1)} %get-tuple-element.42) | copy-start | bytes 12582916
  76.1 12.3 %all-to-all-start.1 = ((bf16[4,2,64,4,128]{4,3,2,1,0:T(4,128)(2,1)}), bf16[4,2,64,4,128]{4,3,2,1,0:T(4,128)(2,1)S(1)}, u32[]{:S(2)}, u32[]{:S(2)}) async-start(bf16[4,2,64,4,128]{4,3,2,1,0:T(4,128)(2,1)} %pad_maximum_fusion), calls=%async_computation.1 | async-start | bytes 1048576 | tf_op jit(solution)/shard_map/all_to_all | solution.py:260
  90.6 13.7 %all-to-all-start.4 = ((bf16[2,64,4,128]{3,2,0,1:T(4,128)(2,1)}), bf16[2,64,4,128]{3,2,0,1:T(4,128)(2,1)S(1)}, u32[]{:S(2)}, u32[]{:S(2)}) async-start(bf16[2,64,4,128]{3,2,0,1:T(4,128)(2,1)} %copy.75), calls=%async_computation.4 | async-start | bytes 262144 | tf_op jit(solution)/shard_map/all_to_all | solution.py:317
  94.0 8.2 %copy-start.1 = (bf16[16,1024,128]{2,1,0:T(8,128)(2,1)S(1)}, bf16[16,1024,128]{2,1,0:T(8,128)(2,1)}, u32[]{:S(2)}) copy-start(bf16[16,1024,128]{2,1,0:T(8,128)(2,1)} %get-tuple-element.42) | copy-start | bytes 12582916
  104.3 26.3 %all-to-all-start.3 = ((bf16[32,8,1024]{2,1,0:T(8,128)(2,1)}), bf16[32,8,1024]{2,1,0:T(8,128)(2,1)S(1)}, u32[]{:S(2)}, u32[]{:S(2)}) async-start(bf16[32,8,1024]{2,1,0:T(8,128)(2,1)} %fusion.2), calls=%async_computation.3 | async-start | bytes 1048576 | tf_op jit(solution)/shard_map/all_to_all | solution.py:300
Sparse Core Ops, SparseCore 0:
  27.6 40.5 all-gather.3

commit v2 on v0

--- a/solution.py
+++ b/solution.py
@@ -1,6 +1,10 @@
+import functools
+
 import jax
 import jax.numpy as jnp
 from jax import lax
+from jax.experimental import pallas as pl
+from jax.experimental.pallas import tpu as pltpu
 from jax.sharding import PartitionSpec as P
 
 E = 4
@@ -196,9 +200,402 @@
     )
 
 
+def fused_kernel(
+    sizes,
+    tok,
+    cot,
+    q_in,
+    k_in,
+    routes_in,
+    value_hbm,
+    output_hbm,
+    tok_out,
+    qg_out,
+    kg_out,
+    vg_out,
+    og_out,
+    rows,
+    flat,
+    flat_t,
+    routes,
+    weight,
+    heads_in,
+    part,
+    part_in,
+    factor,
+    masked,
+    score_keep,
+    back,
+    back_in,
+    term,
+    term_in,
+    grads,
+    sem_weight,
+    sem_own,
+    sem_rows,
+    sem_routes,
+    sem_line,
+    sem_side,
+    sem_heads,
+    sem_part,
+    sem_factor,
+    sem_back,
+    sem_term,
+    sem_grads,
+):
+    dn, gn, jn, own_heads, query_rows, tok_rows, width, head_dim = sizes
+    sources = gn * jn
+    seq_len = sources * tok_rows
+    scale = head_dim ** (-0.5)
+    d, g, j = lax.axis_index("dp"), lax.axis_index("head"), lax.axis_index("expert")
+    block = g * jn + j
+    f32, bf16 = jnp.float32, jnp.bfloat16
+
+    def at(dd, gg, jj):
+        return {"dp": lax.rem(d + dd, dn), "head": lax.rem(g + gg, gn), "expert": lax.rem(j + jj, jn)}
+
+    others = [
+        (dd, gg, jj)
+        for dd in range(dn)
+        for gg in range(gn)
+        for jj in range(jn)
+        if (dd, gg, jj) != (0, 0, 0)
+    ]
+    sent = []
+
+    def send(src, dst, sems, slot, where):
+        copy = pltpu.make_async_remote_copy(
+            src_ref=src,
+            dst_ref=dst,
+            send_sem=sems.at[(0,) + slot],
+            recv_sem=sems.at[(1,) + slot],
+            device_id=at(*where),
+            device_id_type=pl.DeviceIdType.MESH,
+        )
+        copy.start()
+        sent.append(copy)
+        return copy
+
+    def columns(index):
+        return pl.ds(pl.multiple_of(index * width, 128), width)
+
+    weights_on_way = [
+        pltpu.make_async_copy(hbm.at[:, columns(d), :], weight.at[i], sem_weight.at[i])
+        for i, hbm in enumerate((value_hbm, output_hbm))
+    ]
+    for copy in weights_on_way:
+        copy.start()
+    own = [
+        pltpu.make_async_copy(tok.at[:, columns(d)], rows.at[block, 0, d], sem_own.at[0]),
+        pltpu.make_async_copy(cot.at[:, columns(d)], rows.at[block, 1, d], sem_own.at[1]),
+        pltpu.make_async_copy(routes_in, routes.at[d], sem_own.at[2]),
+        pltpu.make_async_copy(q_in.at[j], heads_in.at[0, j], sem_own.at[3]),
+        pltpu.make_async_copy(k_in.at[j], heads_in.at[1, j], sem_own.at[4]),
+    ]
+    for copy in own:
+        copy.start()
+
+    barrier = pltpu.get_barrier_semaphore()
+    for where in others:
+        pl.semaphore_signal(
+            barrier, inc=1, device_id=at(*where), device_id_type=pl.DeviceIdType.MESH
+        )
+    pl.semaphore_wait(barrier, len(others))
+
+    first = []
+    for dd in range(1, dn):
+        target = columns(lax.rem(d + dd, dn))
+        first.append(send(tok.at[:, target], rows.at[block, 0, d], sem_rows, (dd, 0), (dd, 0, 0)))
+        first.append(send(cot.at[:, target], rows.at[block, 1, d], sem_rows, (dd, 1), (dd, 0, 0)))
+    for copy in own:
+        copy.wait()
+    for copy in first:
+        copy.wait_recv()
+    line = [
+        send(rows.at[block], rows.at[block], sem_line, (gg,), (0, gg, 0)) for gg in range(1, gn)
+    ]
+    side = [
+        send(rows.at[block], rows.at[block], sem_side, (0, jj), (0, 0, jj)) for jj in range(1, jn)
+    ]
+    late = [
+        send(routes_in, routes.at[d], sem_routes, (dd,), (dd, 0, 0)) for dd in range(1, dn)
+    ]
+    for jj in range(1, jn):
+        peer = lax.rem(j + jj, jn)
+        late.append(send(q_in.at[peer], heads_in.at[0, j], sem_heads, (0, jj), (0, 0, jj)))
+        late.append(send(k_in.at[peer], heads_in.at[1, j], sem_heads, (1, jj), (0, 0, jj)))
+    for gg in range(1, gn):
+        line[gg - 1].wait_recv()
+        came = lax.rem(g + gn - gg, gn) * jn + j
+        for jj in range(1, jn):
+            side.append(send(rows.at[came], rows.at[came], sem_side, (gg, jj), (0, 0, jj)))
+    for copy in side + late:
+        copy.wait_recv()
+
+    for i in range(2):
+        for b in range(dn):
+            piece = jnp.concatenate([rows[s, i, b].astype(f32) for s in range(sources)], axis=0)
+            flat[i, b * seq_len : (b + 1) * seq_len, :] = piece.astype(bf16)
+    for copy in weights_on_way:
+        copy.wait()
+
+    def column(i, h, b):
+        c = i * own_heads + h
+        return jnp.broadcast_to(routes[b, :, c : c + 1], (seq_len, head_dim))
+
+    for i in range(2):
+        for h in range(own_heads):
+            picked = [jnp.zeros((seq_len, head_dim), f32) for _ in range(dn)]
+            for e in range(0, E, 2):
+                p = h * E + e
+                both = jnp.concatenate([weight[i, p], weight[i, p + 1]], axis=1)
+                every = jnp.dot(flat[i], both, preferred_element_type=f32)
+                for b in range(dn):
+                    own_rows = every[b * seq_len : (b + 1) * seq_len]
+                    route = column(i, h, b)
+                    picked[b] = jnp.where(route == e, own_rows[:, :head_dim], picked[b])
+                    picked[b] = jnp.where(route == e + 1, own_rows[:, head_dim:], picked[b])
+            for b in range(dn):
+                part[b, i, h] = picked[b].astype(bf16)
+    summed = [
+        send(part.at[lax.rem(d + dd, dn)], part_in.at[dd], sem_part, (dd,), (dd, 0, 0))
+        for dd in range(1, dn)
+    ]
+    for i in range(2):
+        flat_t[i] = flat[i].T
+    for copy in summed:
+        copy.wait_recv()
+
+    query_pos = lax.broadcasted_iota(jnp.int32, (seq_len, seq_len), 0)
+    key_pos = lax.broadcasted_iota(jnp.int32, (seq_len, seq_len), 1)
+    causal = key_pos <= query_pos
+
+    def joined(i, h):
+        return jnp.concatenate([heads_in[i, jj, h] for jj in range(jn)], axis=0)
+
+    def total(i, h):
+        whole = part[d, i, h].astype(f32)
+        for dd in range(1, dn):
+            whole = whole + part_in[dd, i, h].astype(f32)
+        return whole.astype(bf16)
+
+    def across(a, b):
+        return lax.dot_general(a, b, (((1,), (1,)), ((), ())), preferred_element_type=f32)
+
+    def over_rows(a, b):
+        return lax.dot_general(a, b, (((0,), (0,)), ((), ())), preferred_element_type=f32)
+
+    for h in range(own_heads):
+        query, key = joined(0, h), joined(1, h)
+        value, upstream = total(0, h), total(1, h)
+        scores = across(query, key) * scale
+        top = jnp.max(jnp.where(causal, scores, -jnp.inf), axis=-1, keepdims=True)
+        soft = jnp.where(causal, jnp.exp(scores - top), 0.0)
+        probs = soft / jnp.sum(soft, axis=-1, keepdims=True)
+        half = probs.astype(bf16)
+        output = jnp.dot(half, value, preferred_element_type=f32).astype(bf16)
+        factor[d, 0, h] = over_rows(half, upstream).astype(bf16)
+        factor[d, 1, h] = output
+        delta = jnp.sum(output.astype(f32) * upstream.astype(f32), axis=-1, keepdims=True)
+        score_keep[h] = (probs * (across(upstream, value) - delta)).astype(bf16)
+    spread = [
+        send(factor.at[d], factor.at[d], sem_factor, (dd,), (dd, 0, 0)) for dd in range(1, dn)
+    ]
+    for h in range(own_heads):
+        query, key, score = joined(0, h), joined(1, h), score_keep[h]
+        query_grad = (jnp.dot(score, key, preferred_element_type=f32) * scale).astype(bf16)
+        key_grad = (over_rows(score, query) * scale).astype(bf16)
+        for jj in range(jn):
+            back[jj, 0, h] = query_grad[jj * query_rows : (jj + 1) * query_rows]
+            back[jj, 1, h] = key_grad[jj * query_rows : (jj + 1) * query_rows]
+    returned = [
+        send(back.at[lax.rem(j + jj, jn)], back_in.at[j], sem_back, (jj,), (0, 0, jj))
+        for jj in range(1, jn)
+    ]
+    for copy in spread:
+        copy.wait_recv()
+
+    for i in range(2):
+        for h in range(own_heads):
+            for b in range(dn):
+                source = factor[b, i, h].astype(f32)
+                route = column(i, h, b)
+                for e in range(E):
+                    p = h * E + e
+                    masked[
+                        i,
+                        p // 2,
+                        b * seq_len : (b + 1) * seq_len,
+                        (p % 2) * head_dim : (p % 2 + 1) * head_dim,
+                    ] = jnp.where(route == e, source, 0.0).astype(bf16)
+    couples = own_heads * E // 2
+    step = min(width, 256)
+    for n in range(0, width, step):
+        added = jnp.zeros((dn * seq_len, step), f32)
+        for c in range(couples):
+            both = jnp.concatenate(
+                [weight[0, 2 * c, n : n + step, :], weight[0, 2 * c + 1, n : n + step, :]], axis=1
+            )
+            added = added + across(masked[0, c], both)
+        for r in range(dn * sources):
+            term[r, :, n : n + step] = added[r * tok_rows : (r + 1) * tok_rows].astype(bf16)
+    terms = []
+    for slot, (dd, gg, jj) in enumerate(others):
+        target = (
+            lax.rem(d + dd, dn) * sources + lax.rem(g + gg, gn) * jn + lax.rem(j + jj, jn)
+        )
+        terms.append(
+            send(term.at[target], term_in.at[d * sources + block], sem_term, (slot,), (dd, gg, jj))
+        )
+    term_in[d * sources + block] = term[d * sources + block]
+
+    for i, out in enumerate((vg_out, og_out)):
+
+        def one(c, carry, i=i, out=out):
+            whole = jnp.dot(flat_t[i], masked[i, c], preferred_element_type=f32).astype(bf16)
+            grads[i, 2 * c] = whole[:, :head_dim]
+            grads[i, 2 * c + 1] = whole[:, head_dim:]
+            pltpu.make_async_copy(
+                grads.at[i, pl.ds(2 * c, 2)], out.at[pl.ds(2 * c, 2)], sem_grads.at[i, c]
+            ).start()
+            return carry
+
+        lax.fori_loop(0, couples, one, 0)
+
+    back_in[j] = back[j]
+    for copy in returned:
+        copy.wait_recv()
+    for jj in range(jn):
+        qg_out[jj] = back_in[jj, 0]
+        kg_out[jj] = back_in[jj, 1]
+    for copy in terms:
+        copy.wait_recv()
+    for b in range(dn):
+        total_rows = term_in[b * sources].astype(f32)
+        for s in range(1, sources):
+            total_rows = total_rows + term_in[b * sources + s].astype(f32)
+        tok_out[:, b * width : (b + 1) * width] = total_rows.astype(bf16)
+    for i, out in enumerate((vg_out, og_out)):
+        for c in range(couples):
+            pltpu.make_async_copy(
+                grads.at[i, pl.ds(2 * c, 2)], out.at[pl.ds(2 * c, 2)], sem_grads.at[i, c]
+            ).wait()
+    for copy in sent:
+        copy.wait_send()
+
+
+def fused(
+    tokens,
+    cotangent,
+    queries,
+    key_vectors,
+    value_routes,
+    output_routes,
+    value_experts,
+    output_experts,
+):
+    dn, gn, jn = lax.axis_size("dp"), lax.axis_size("head"), lax.axis_size("expert")
+    expert_index = lax.axis_index("expert")
+    _, tok_rows, model_width = tokens.shape
+    width = model_width // dn
+    _, query_rows, groups, head_dim = queries.shape
+    seq_len = value_routes.shape[2]
+    pairs_dev = value_experts.shape[0]
+    own_heads = groups // jn
+    sources = gn * jn
+    bf16 = jnp.bfloat16
+
+    routes = jnp.concatenate(
+        [
+            lax.dynamic_slice_in_dim(route[0, :, :, 0], expert_index * own_heads, own_heads, 0)
+            for route in (value_routes, output_routes)
+        ]
+    )
+    routes = jnp.pad(routes.T, ((0, 0), (0, 128 - 2 * own_heads)))
+
+    def by_head(x):
+        return x[0].transpose(1, 0, 2).reshape(jn, own_heads, query_rows, head_dim)
+
+    vmem = pl.BlockSpec(memory_space=pltpu.VMEM)
+    hbm = pl.BlockSpec(memory_space=pl.ANY)
+    dma = pltpu.SemaphoreType.DMA
+    head_block = (jn, own_heads, query_rows, head_dim)
+    grad_shape = jax.ShapeDtypeStruct((pairs_dev, width, head_dim), bf16)
+    tok_grads, query_grads, key_grads, value_grads, output_grads = pl.pallas_call(
+        functools.partial(
+            fused_kernel, (dn, gn, jn, own_heads, query_rows, tok_rows, width, head_dim)
+        ),
+        name="fused",
+        out_shape=(
+            jax.ShapeDtypeStruct((tok_rows, model_width), bf16),
+            jax.ShapeDtypeStruct(head_block, bf16),
+            jax.ShapeDtypeStruct(head_block, bf16),
+            grad_shape,
+            grad_shape,
+        ),
+        in_specs=[vmem] * 5 + [hbm] * 2,
+        out_specs=(vmem, vmem, vmem, hbm, hbm),
+        scratch_shapes=[
+            pltpu.VMEM((sources, 2, dn, tok_rows, width), bf16),
+            pltpu.VMEM((2, dn * seq_len, width), bf16),
+            pltpu.VMEM((2, width, dn * seq_len), bf16),
+            pltpu.VMEM((dn, seq_len, 128), jnp.int32),
+            pltpu.VMEM((2, pairs_dev, width, head_dim), bf16),
+            pltpu.VMEM((2, jn, own_heads, query_rows, head_dim), bf16),
+            pltpu.VMEM((dn, 2, own_heads, seq_len, head_dim), bf16),
+            pltpu.VMEM((dn, 2, own_heads, seq_len, head_dim), bf16),
+            pltpu.VMEM((dn, 2, own_heads, seq_len, head_dim), bf16),
+            pltpu.VMEM((2, pairs_dev // 2, dn * seq_len, 2 * head_dim), bf16),
+            pltpu.VMEM((own_heads, seq_len, seq_len), bf16),
+            pltpu.VMEM((jn, 2, own_heads, query_rows, head_dim), bf16),
+            pltpu.VMEM((jn, 2, own_heads, query_rows, head_dim), bf16),
+            pltpu.VMEM((dn * sources, tok_rows, width), bf16),
+            pltpu.VMEM((dn * sources, tok_rows, width), bf16),
+            pltpu.VMEM((2, pairs_dev, width, head_dim), bf16),
+            dma((2,)),
+            dma((5,)),
+            dma((2, dn, 2)),
+            dma((2, dn)),
+            dma((2, gn)),
+            dma((2, gn, jn)),
+            dma((2, 2, jn)),
+            dma((2, dn)),
+            dma((2, dn)),
+            dma((2, jn)),
+            dma((2, dn * sources)),
+            dma((2, pairs_dev // 2)),
+        ],
+        compiler_params=pltpu.CompilerParams(
+            collective_id=0, has_side_effects=True, vmem_limit_bytes=60 * 1024 * 1024
+        ),
+    )(
+        tokens[0],
+        cotangent[0],
+        by_head(queries),
+        by_head(key_vectors),
+        routes,
+        value_experts,
+        output_experts,
+    )
+
+    def by_row(x):
+        return x.reshape(groups, query_rows, head_dim).transpose(1, 0, 2)[None]
+
+    return tok_grads[None], by_row(query_grads), by_row(key_grads), value_grads, output_grads
+
+
+def chosen(*args):
+    groups, pairs_dev = args[2].shape[2], args[6].shape[0]
+    dp_count, expert_count = lax.axis_size("dp"), lax.axis_size("expert")
+    whole_heads = groups % expert_count == 0 and pairs_dev == groups // expert_count * E
+    if whole_heads and args[0].shape[2] % (dp_count * 256) == 0 and args[2].shape[1] <= 64:
+        return fused(*args)
+    return local(*args)
+
+
 def solution(mesh):
     return jax.shard_map(
-        local,
+        chosen,
         mesh=mesh,
         in_specs=(
             P("dp", ("head", "expert"), None),

time: 426 us -> 78.8 us (0.18)
  waiting for transfers between devices: 199 us -> 0 us
  blocking collectives: 87.4 us -> 0 us
  matrix products: 67.6 us -> 0 us
  Pallas kernels: 0 us -> 62.2 us
  other arithmetic: 23.7 us -> 0.01 us
  between operations: 14.3 us -> 0.65 us
  starting transfers between devices: 13.1 us -> 0 us
    reduce_scatter x4 -> x0, waiting for transfers between devices: 150 us -> none  [the longest x1 128 us: local(): lax.psum_scatter(value_term.astype(jnp.bfloat16), 'dp', scatter_dimension...]
    all_gather x5 -> x0, blocking collectives: 80.6 us -> none  [the longest x1 32.5 us: local(): lax.all_gather(cotangent[0], ('head', 'expert'), axis=0, tiled=True)]
    dot_general x16 -> x0, matrix products: 67.6 us -> none  [the longest x1 15.1 us: local(): jnp.einsum('prk,pwk->prw', grad_slots, value_experts, preferred_element_t...]
    pallas_call x0 -> x1, Pallas kernels: none -> 62.2 us  [fused(): pl.pallas_call(functools.partial(fused_kernel, (dn, gn, jn, own_heads, qu...]
    all_to_all x3 -> x0, waiting for transfers between devices: 49.7 us -> none  [the longest x1 47.7 us: local(): lax.all_to_all(token_terms.reshape(pairs_dev, sources, CAP, model_width),...]
    another operation x5 -> x0, other arithmetic: 15.4 us -> none  [slot_rank(): before = jnp.cumsum(onehot, axis=-2) - onehot]
    all_to_all x3 -> x0, starting transfers between devices: 12.7 us -> none  [the longest x1 5.3 us: local(): lax.all_to_all(token_terms.reshape(pairs_dev, sources, CAP, model_width),...]
    all_to_all x1 -> x0, blocking collectives: 6.85 us -> none  [local(): lax.all_to_all(value_send, 'expert', split_axis=0, concat_axis=1, tiled=T...]
  transfers between devices with their start and end apart: 7 -> 0, of which waited for: 4 -> 0; matrix products, arithmetic and copies ran while one was open for 20% -> 0% of each run, Pallas kernels for 0% -> 0%
where the time goes in v2:
time: 78.8 us; the launch traced here: 78.4 us
  Pallas kernels  62.2 us (79%)
  local copies, waits for them, and re-layouts  15.6 us (20%)
    pallas_call x1, Pallas kernels, fused(): pl.pallas_call(functools.partial(fused_kernel, (dn, gn, jn, own_heads, qu...  62.2 us
    unnamed x5, local copies, waits for them, and re-layouts  8.24 us
    reshape x2, local copies, waits for them, and re-layouts, by_row(): return x.reshape(groups, query_rows, head_dim).transpose(1, 0, 2)[None]  2.99 us
    transpose x2, local copies, waits for them, and re-layouts, by_head(): return x[0].transpose(1, 0, 2).reshape(jn, own_heads, query_rows, head_dim)  2.96 us

profile of v2, /device:TPU:0, one launch (start us, length us, event | category | flops | bytes accessed | tf_op | source)
XLA Modules:
  0.0 78.4 jit_solution(4166950583021719489)
XLA Ops:
  0.6 0.7 constant_dynamic-slice_fusion
  1.4 0.1 copy.21
  1.4 0.6 pad.4.routes_in
  2.1 1.5 %copy.19 = bf16[8,32,128]{2,1,0:T(8,128)(2,1)} copy(bf16[8,32,128]{2,0,1:T(8,128)(2,1)} %bitcast.31) | data formatting | bytes 131072 | tf_op jit(solution)/shard_map/transpose | solution.py:517
  3.5 1.5 %copy.20 = bf16[8,32,128]{2,1,0:T(8,128)(2,1)} copy(bf16[8,32,128]{2,0,1:T(8,128)(2,1)} %bitcast.32) | data formatting | bytes 131072 | tf_op jit(solution)/shard_map/transpose | solution.py:517
  5.0 62.2 %fused.1 = (bf16[8,4096]{1,0:T(8,128)(2,1)}, bf16[2,4,32,128]{3,2,1,0:T(8,128)(2,1)}, bf16[2,4,32,128]{3,2,1,0:T(8,128)(2,1)}, bf16[16,1024,128]{2,1,0:T(8,128)(2,1)}, bf16[16,1024,128]{2,1,0:T(8,128)(2,1)}) custom-call(bf16[8,4096]{1,0:T(8,128)(2,1)} %bitcast.29, bf16[8,4096]{1,0:T(8,128)(2,1)} %bitcast.30, bf16[2,4,32,128]{3,2,1,0:T(8,128)(2,1)} %bitcast.26, ...), custom_call_target="tpu_custom_call" | custom-call | tf_op jit(solution)/shard_map/fused/pallas_call | solution.py:524
  67.2 1.5 %copy.27 = bf16[8,32,128]{2,0,1:T(8,128)(2,1)} copy(bf16[8,32,128]{2,1,0:T(8,128)(2,1)} %bitcast.37) | data formatting | bytes 131072 | tf_op jit(solution)/shard_map/reshape | solution.py:582
  68.7 1.5 %copy.26 = bf16[8,32,128]{2,0,1:T(8,128)(2,1)} copy(bf16[8,32,128]{2,1,0:T(8,128)(2,1)} %bitcast.36) | data formatting | bytes 131072 | tf_op jit(solution)/shard_map/reshape | solution.py:582
  70.2 1.5 %copy.31 = bf16[1,8,4096]{2,1,0:T(8,128)(2,1)} copy(bf16[1,8,4096]{2,1,0:T(8,128)(2,1)} %bitcast.35) | data formatting | bytes 131072
  71.7 0.0 copy-start
  71.7 4.8 %copy.32 = bf16[16,1024,128]{2,1,0:T(8,128)(2,1)} copy(bf16[16,1024,128]{2,1,0:T(8,128)(2,1)} %get-tuple-element.25) | data formatting | bytes 8388608
  76.4 0.0 copy-done
  76.4 2.0 %copy.33 = bf16[16,1024,128]{2,1,0:T(8,128)(2,1)} copy(bf16[16,1024,128]{2,1,0:T(8,128)(2,1)S(1)} %copy-done) | data formatting | bytes 8388608
  (1 shorter events, 0.0 us)
Async XLA Ops:
  71.7 4.8 %copy-start = (bf16[16,1024,128]{2,1,0:T(8,128)(2,1)S(1)}, bf16[16,1024,128]{2,1,0:T(8,128)(2,1)}, u32[]{:S(2)}) copy-start(bf16[16,1024,128]{2,1,0:T(8,128)(2,1)} %get-tuple-element.26) | copy-start | bytes 12582916

commit v3 on v2

--- a/solution.py
+++ b/solution.py
@@ -212,11 +212,12 @@
     tok_out,
     qg_out,
     kg_out,
-    vg_out,
-    og_out,
+    flat_out,
+    masked_out,
     rows,
     flat,
     flat_t,
+    by_heads,
     routes,
     weight,
     heads_in,
@@ -225,11 +226,12 @@
     factor,
     masked,
     score_keep,
+    prob_keep,
+    upstream_keep,
     back,
     back_in,
     term,
     term_in,
-    grads,
     sem_weight,
     sem_own,
     sem_rows,
@@ -289,8 +291,6 @@
         pltpu.make_async_copy(tok.at[:, columns(d)], rows.at[block, 0, d], sem_own.at[0]),
         pltpu.make_async_copy(cot.at[:, columns(d)], rows.at[block, 1, d], sem_own.at[1]),
         pltpu.make_async_copy(routes_in, routes.at[d], sem_own.at[2]),
-        pltpu.make_async_copy(q_in.at[j], heads_in.at[0, j], sem_own.at[3]),
-        pltpu.make_async_copy(k_in.at[j], heads_in.at[1, j], sem_own.at[4]),
     ]
     for copy in own:
         copy.start()
@@ -302,48 +302,62 @@
         )
     pl.semaphore_wait(barrier, len(others))
 
-    first = []
-    for dd in range(1, dn):
-        target = columns(lax.rem(d + dd, dn))
-        first.append(send(tok.at[:, target], rows.at[block, 0, d], sem_rows, (dd, 0), (dd, 0, 0)))
-        first.append(send(cot.at[:, target], rows.at[block, 1, d], sem_rows, (dd, 1), (dd, 0, 0)))
+    first, late, line, side = [[], []], [], [[], []], [[], []]
+    for i in (1, 0):
+        for dd in range(1, dn):
+            target = columns(lax.rem(d + dd, dn))
+            source = (tok, cot)[i]
+            first[i].append(
+                send(source.at[:, target], rows.at[block, i, d], sem_rows, (dd, i), (dd, 0, 0))
+            )
+        if i == 1:
+            late = [
+                send(routes_in, routes.at[d], sem_routes, (dd,), (dd, 0, 0))
+                for dd in range(1, dn)
+            ]
     for copy in own:
         copy.wait()
-    for copy in first:
-        copy.wait_recv()
-    line = [
-        send(rows.at[block], rows.at[block], sem_line, (gg,), (0, gg, 0)) for gg in range(1, gn)
-    ]
-    side = [
-        send(rows.at[block], rows.at[block], sem_side, (0, jj), (0, 0, jj)) for jj in range(1, jn)
-    ]
-    late = [
-        send(routes_in, routes.at[d], sem_routes, (dd,), (dd, 0, 0)) for dd in range(1, dn)
-    ]
+    for i in (1, 0):
+        for copy in first[i]:
+            copy.wait_recv()
+        here = rows.at[block, i]
+        for gg in range(1, gn):
+            line[i].append(send(here, here, sem_line, (gg, i), (0, gg, 0)))
+        for jj in range(1, jn):
+            side[i].append(send(here, here, sem_side, (0, jj, i), (0, 0, jj)))
+    for i, source in enumerate((q_in, k_in)):
+        turned = jnp.transpose(source[...].astype(f32), (1, 0, 2)).astype(bf16)
+        for jj in range(jn):
+            by_heads[i, jj] = turned[jj * own_heads : (jj + 1) * own_heads]
+        heads_in[i, j] = by_heads[i, j]
+    swapped = []
     for jj in range(1, jn):
         peer = lax.rem(j + jj, jn)
-        late.append(send(q_in.at[peer], heads_in.at[0, j], sem_heads, (0, jj), (0, 0, jj)))
-        late.append(send(k_in.at[peer], heads_in.at[1, j], sem_heads, (1, jj), (0, 0, jj)))
-    for gg in range(1, gn):
-        line[gg - 1].wait_recv()
-        came = lax.rem(g + gn - gg, gn) * jn + j
-        for jj in range(1, jn):
-            side.append(send(rows.at[came], rows.at[came], sem_side, (gg, jj), (0, 0, jj)))
-    for copy in side + late:
-        copy.wait_recv()
-
-    for i in range(2):
+        for i in range(2):
+            swapped.append(
+                send(by_heads.at[i, peer], heads_in.at[i, j], sem_heads, (i, jj), (0, 0, jj))
+            )
+
+    def forward(i):
+        for gg in range(1, gn):
+            line[i][gg - 1].wait_recv()
+            came = rows.at[lax.rem(g + gn - gg, gn) * jn + j, i]
+            for jj in range(1, jn):
+                side[i].append(send(came, came, sem_side, (gg, jj, i), (0, 0, jj)))
+
+    def flatten(i):
+        for copy in side[i]:
+            copy.wait_recv()
         for b in range(dn):
             piece = jnp.concatenate([rows[s, i, b].astype(f32) for s in range(sources)], axis=0)
             flat[i, b * seq_len : (b + 1) * seq_len, :] = piece.astype(bf16)
-    for copy in weights_on_way:
-        copy.wait()
 
     def column(i, h, b):
         c = i * own_heads + h
         return jnp.broadcast_to(routes[b, :, c : c + 1], (seq_len, head_dim))
 
-    for i in range(2):
+    def project(i):
+        weights_on_way[i].wait()
         for h in range(own_heads):
             picked = [jnp.zeros((seq_len, head_dim), f32) for _ in range(dn)]
             for e in range(0, E, 2):
@@ -357,14 +371,19 @@
                     picked[b] = jnp.where(route == e + 1, own_rows[:, head_dim:], picked[b])
             for b in range(dn):
                 part[b, i, h] = picked[b].astype(bf16)
-    summed = [
-        send(part.at[lax.rem(d + dd, dn)], part_in.at[dd], sem_part, (dd,), (dd, 0, 0))
-        for dd in range(1, dn)
-    ]
-    for i in range(2):
-        flat_t[i] = flat[i].T
-    for copy in summed:
-        copy.wait_recv()
+        return [
+            send(
+                part.at[lax.rem(d + dd, dn), i], part_in.at[dd, i], sem_part, (dd, i), (dd, 0, 0)
+            )
+            for dd in range(1, dn)
+        ]
+
+    forward(1)
+    flatten(1)
+    for copy in late:
+        copy.wait_recv()
+    upstream_on_way = project(1)
+    forward(0)
 
     query_pos = lax.broadcasted_iota(jnp.int32, (seq_len, seq_len), 0)
     key_pos = lax.broadcasted_iota(jnp.int32, (seq_len, seq_len), 1)
@@ -385,37 +404,7 @@
     def over_rows(a, b):
         return lax.dot_general(a, b, (((0,), (0,)), ((), ())), preferred_element_type=f32)
 
-    for h in range(own_heads):
-        query, key = joined(0, h), joined(1, h)
-        value, upstream = total(0, h), total(1, h)
-        scores = across(query, key) * scale
-        top = jnp.max(jnp.where(causal, scores, -jnp.inf), axis=-1, keepdims=True)
-        soft = jnp.where(causal, jnp.exp(scores - top), 0.0)
-        probs = soft / jnp.sum(soft, axis=-1, keepdims=True)
-        half = probs.astype(bf16)
-        output = jnp.dot(half, value, preferred_element_type=f32).astype(bf16)
-        factor[d, 0, h] = over_rows(half, upstream).astype(bf16)
-        factor[d, 1, h] = output
-        delta = jnp.sum(output.astype(f32) * upstream.astype(f32), axis=-1, keepdims=True)
-        score_keep[h] = (probs * (across(upstream, value) - delta)).astype(bf16)
-    spread = [
-        send(factor.at[d], factor.at[d], sem_factor, (dd,), (dd, 0, 0)) for dd in range(1, dn)
-    ]
-    for h in range(own_heads):
-        query, key, score = joined(0, h), joined(1, h), score_keep[h]
-        query_grad = (jnp.dot(score, key, preferred_element_type=f32) * scale).astype(bf16)
-        key_grad = (over_rows(score, query) * scale).astype(bf16)
-        for jj in range(jn):
-            back[jj, 0, h] = query_grad[jj * query_rows : (jj + 1) * query_rows]
-            back[jj, 1, h] = key_grad[jj * query_rows : (jj + 1) * query_rows]
-    returned = [
-        send(back.at[lax.rem(j + jj, jn)], back_in.at[j], sem_back, (jj,), (0, 0, jj))
-        for jj in range(1, jn)
-    ]
-    for copy in spread:
-        copy.wait_recv()
-
-    for i in range(2):
+    def mask(i):
         for h in range(own_heads):
             for b in range(dn):
                 source = factor[b, i, h].astype(f32)
@@ -428,6 +417,32 @@
                         b * seq_len : (b + 1) * seq_len,
                         (p % 2) * head_dim : (p % 2 + 1) * head_dim,
                     ] = jnp.where(route == e, source, 0.0).astype(bf16)
+
+    def spread(i):
+        return [
+            send(factor.at[d, i], factor.at[d, i], sem_factor, (dd, i), (dd, 0, 0))
+            for dd in range(1, dn)
+        ]
+
+    for copy in swapped:
+        copy.wait_recv()
+    for h in range(own_heads):
+        query, key = joined(0, h), joined(1, h)
+        scores = across(query, key) * scale
+        top = jnp.max(jnp.where(causal, scores, -jnp.inf), axis=-1, keepdims=True)
+        soft = jnp.where(causal, jnp.exp(scores - top), 0.0)
+        prob_keep[h] = soft / jnp.sum(soft, axis=-1, keepdims=True)
+    for copy in upstream_on_way:
+        copy.wait_recv()
+    for h in range(own_heads):
+        upstream_keep[h] = total(1, h)
+        factor[d, 0, h] = over_rows(prob_keep[h].astype(bf16), upstream_keep[h]).astype(bf16)
+    value_spread = spread(0)
+    flatten(0)
+    values_on_way = project(0)
+    for copy in value_spread:
+        copy.wait_recv()
+    mask(0)
     couples = own_heads * E // 2
     step = min(width, 256)
     for n in range(0, width, step):
@@ -449,18 +464,37 @@
         )
     term_in[d * sources + block] = term[d * sources + block]
 
-    for i, out in enumerate((vg_out, og_out)):
-
-        def one(c, carry, i=i, out=out):
-            whole = jnp.dot(flat_t[i], masked[i, c], preferred_element_type=f32).astype(bf16)
-            grads[i, 2 * c] = whole[:, :head_dim]
-            grads[i, 2 * c + 1] = whole[:, head_dim:]
-            pltpu.make_async_copy(
-                grads.at[i, pl.ds(2 * c, 2)], out.at[pl.ds(2 * c, 2)], sem_grads.at[i, c]
-            ).start()
-            return carry
-
-        lax.fori_loop(0, couples, one, 0)
+    for copy in values_on_way:
+        copy.wait_recv()
+    for h in range(own_heads):
+        value, upstream, probs = total(0, h), upstream_keep[h], prob_keep[h]
+        output = jnp.dot(probs.astype(bf16), value, preferred_element_type=f32).astype(bf16)
+        factor[d, 1, h] = output
+        delta = jnp.sum(output.astype(f32) * upstream.astype(f32), axis=-1, keepdims=True)
+        score_keep[h] = (probs * (across(upstream, value) - delta)).astype(bf16)
+    output_spread = spread(1)
+    for h in range(own_heads):
+        query, key, score = joined(0, h), joined(1, h), score_keep[h]
+        query_grad = (jnp.dot(score, key, preferred_element_type=f32) * scale).astype(bf16)
+        key_grad = (over_rows(score, query) * scale).astype(bf16)
+        for jj in range(jn):
+            back[jj, 0, h] = query_grad[jj * query_rows : (jj + 1) * query_rows]
+            back[jj, 1, h] = key_grad[jj * query_rows : (jj + 1) * query_rows]
+    returned = [
+        send(back.at[lax.rem(j + jj, jn)], back_in.at[j], sem_back, (jj,), (0, 0, jj))
+        for jj in range(1, jn)
+    ]
+    for i in range(2):
+        flat_t[i] = flat[i].T
+    for copy in output_spread:
+        copy.wait_recv()
+    mask(1)
+    outgoing = [
+        pltpu.make_async_copy(flat_t, flat_out, sem_grads.at[0]),
+        pltpu.make_async_copy(masked, masked_out, sem_grads.at[1]),
+    ]
+    for copy in outgoing:
+        copy.start()
 
     back_in[j] = back[j]
     for copy in returned:
@@ -475,13 +509,24 @@
         for s in range(1, sources):
             total_rows = total_rows + term_in[b * sources + s].astype(f32)
         tok_out[:, b * width : (b + 1) * width] = total_rows.astype(bf16)
-    for i, out in enumerate((vg_out, og_out)):
-        for c in range(couples):
-            pltpu.make_async_copy(
-                grads.at[i, pl.ds(2 * c, 2)], out.at[pl.ds(2 * c, 2)], sem_grads.at[i, c]
-            ).wait()
+    for copy in outgoing:
+        copy.wait()
     for copy in sent:
         copy.wait_send()
+
+
+def finish_kernel(flat_t, masked, tok_in, qg_in, kg_in, tok_out, qg_out, kg_out, vg_out, og_out):
+    @pl.when(pl.program_id(0) == 0)
+    def _():
+        tok_out[...] = tok_in[...]
+        for source, out in ((qg_in, qg_out), (kg_in, kg_out)):
+            out[...] = jnp.transpose(source[...].astype(jnp.float32), (1, 0, 2)).astype(out.dtype)
+
+    half = masked.shape[-1] // 2
+    for i, out in enumerate((vg_out, og_out)):
+        whole = jnp.dot(flat_t[i], masked[i, 0], preferred_element_type=jnp.float32)
+        out[0] = whole[:, :half].astype(out.dtype)
+        out[1] = whole[:, half:].astype(out.dtype)
 
 
 def fused(
@@ -513,15 +558,13 @@
     )
     routes = jnp.pad(routes.T, ((0, 0), (0, 128 - 2 * own_heads)))
 
-    def by_head(x):
-        return x[0].transpose(1, 0, 2).reshape(jn, own_heads, query_rows, head_dim)
-
     vmem = pl.BlockSpec(memory_space=pltpu.VMEM)
     hbm = pl.BlockSpec(memory_space=pl.ANY)
     dma = pltpu.SemaphoreType.DMA
     head_block = (jn, own_heads, query_rows, head_dim)
     grad_shape = jax.ShapeDtypeStruct((pairs_dev, width, head_dim), bf16)
-    tok_grads, query_grads, key_grads, value_grads, output_grads = pl.pallas_call(
+    couples, all_rows = pairs_dev // 2, dn * seq_len
+    tok_grads, query_grads, key_grads, flat_t, masked = pl.pallas_call(
         functools.partial(
             fused_kernel, (dn, gn, jn, own_heads, query_rows, tok_rows, width, head_dim)
         ),
@@ -530,8 +573,8 @@
             jax.ShapeDtypeStruct((tok_rows, model_width), bf16),
             jax.ShapeDtypeStruct(head_block, bf16),
             jax.ShapeDtypeStruct(head_block, bf16),
-            grad_shape,
-            grad_shape,
+            jax.ShapeDtypeStruct((2, width, all_rows), bf16),
+            jax.ShapeDtypeStruct((2, couples, all_rows, 2 * head_dim), bf16),
         ),
         in_specs=[vmem] * 5 + [hbm] * 2,
         out_specs=(vmem, vmem, vmem, hbm, hbm),
@@ -539,6 +582,7 @@
             pltpu.VMEM((sources, 2, dn, tok_rows, width), bf16),
             pltpu.VMEM((2, dn * seq_len, width), bf16),
             pltpu.VMEM((2, width, dn * seq_len), bf16),
+            pltpu.VMEM((2, jn, own_heads, query_rows, head_dim), bf16),
             pltpu.VMEM((dn, seq_len, 128), jnp.int32),
             pltpu.VMEM((2, pairs_dev, width, head_dim), bf16),
             pltpu.VMEM((2, jn, own_heads, query_rows, head_dim), bf16),
@@ -547,23 +591,24 @@
             pltpu.VMEM((dn, 2, own_heads, seq_len, head_dim), bf16),
             pltpu.VMEM((2, pairs_dev // 2, dn * seq_len, 2 * head_dim), bf16),
             pltpu.VMEM((own_heads, seq_len, seq_len), bf16),
+            pltpu.VMEM((own_heads, seq_len, seq_len), jnp.float32),
+            pltpu.VMEM((own_heads, seq_len, head_dim), bf16),
             pltpu.VMEM((jn, 2, own_heads, query_rows, head_dim), bf16),
             pltpu.VMEM((jn, 2, own_heads, query_rows, head_dim), bf16),
             pltpu.VMEM((dn * sources, tok_rows, width), bf16),
             pltpu.VMEM((dn * sources, tok_rows, width), bf16),
-            pltpu.VMEM((2, pairs_dev, width, head_dim), bf16),
             dma((2,)),
-            dma((5,)),
+            dma((3,)),
             dma((2, dn, 2)),
             dma((2, dn)),
-            dma((2, gn)),
-            dma((2, gn, jn)),
+            dma((2, gn, 2)),
+            dma((2, gn, jn, 2)),
             dma((2, 2, jn)),
-            dma((2, dn)),
-            dma((2, dn)),
+            dma((2, dn, 2)),
+            dma((2, dn, 2)),
             dma((2, jn)),
             dma((2, dn * sources)),
-            dma((2, pairs_dev // 2)),
+            dma((2,)),
         ],
         compiler_params=pltpu.CompilerParams(
             collective_id=0, has_side_effects=True, vmem_limit_bytes=60 * 1024 * 1024
@@ -571,17 +616,48 @@
     )(
         tokens[0],
         cotangent[0],
-        by_head(queries),
-        by_head(key_vectors),
+        queries[0],
+        key_vectors[0],
         routes,
         value_experts,
         output_experts,
     )
 
-    def by_row(x):
-        return x.reshape(groups, query_rows, head_dim).transpose(1, 0, 2)[None]
-
-    return tok_grads[None], by_row(query_grads), by_row(key_grads), value_grads, output_grads
+    def fixed(shape):
+        return pl.BlockSpec(shape, lambda c: (0,) * len(shape))
+
+    by_head = (groups, query_rows, head_dim)
+    by_row = (query_rows, groups, head_dim)
+    grad_block = pl.BlockSpec((2, width, head_dim), lambda c: (c, 0, 0))
+    row_shape = jax.ShapeDtypeStruct(by_row, bf16)
+    tok_grads, query_grads, key_grads, value_grads, output_grads = pl.pallas_call(
+        finish_kernel,
+        name="finish",
+        grid=(couples,),
+        out_shape=(
+            jax.ShapeDtypeStruct((tok_rows, model_width), bf16),
+            row_shape,
+            row_shape,
+            grad_shape,
+            grad_shape,
+        ),
+        in_specs=[
+            fixed((2, width, all_rows)),
+            pl.BlockSpec((2, 1, all_rows, 2 * head_dim), lambda c: (0, c, 0, 0)),
+            fixed((tok_rows, model_width)),
+            fixed(by_head),
+            fixed(by_head),
+        ],
+        out_specs=(
+            fixed((tok_rows, model_width)),
+            fixed(by_row),
+            fixed(by_row),
+            grad_block,
+            grad_block,
+        ),
+        compiler_params=pltpu.CompilerParams(vmem_limit_bytes=60 * 1024 * 1024),
+    )(flat_t, masked, tok_grads, query_grads.reshape(by_head), key_grads.reshape(by_head))
+    return tok_grads[None], query_grads[None], key_grads[None], value_grads, output_grads
 
 
 def chosen(*args):

time: 78.8 us -> 58.7 us (0.74)
  local copies, waits for them, and re-layouts: 15.6 us -> 1.41 us
  Pallas kernels: 62.2 us -> 56.1 us
    pallas_call x1, Pallas kernels: 62.2 us -> 47.4 us  [fused(): pl.pallas_call(functools.partial(fused_kernel, (dn, gn, jn, own_heads, qu...]
    pallas_call x0 -> x1, Pallas kernels: none -> 8.66 us  [fused(): pl.pallas_call(finish_kernel, name='finish', grid=(couples,), out_shape=(...]
    unnamed x5 -> x0, local copies, waits for them, and re-layouts: 8.24 us -> none
    reshape x2 -> x0, local copies, waits for them, and re-layouts: 2.99 us -> none  [by_row(): return x.reshape(groups, query_rows, head_dim).transpose(1, 0, 2)[None]]
    transpose x2 -> x0, local copies, waits for them, and re-layouts: 2.96 us -> none  [by_head(): return x[0].transpose(1, 0, 2).reshape(jn, own_heads, query_rows, head_dim)]
where the time goes in v3:
time: 58.7 us; the launch traced here: 58.2 us
  Pallas kernels  56.1 us (96%)
  local copies, waits for them, and re-layouts  1.41 us (2%)
  between operations  0.65 us (1%)
    pallas_call x1, Pallas kernels, fused(): pl.pallas_call(functools.partial(fused_kernel, (dn, gn, jn, own_heads, qu...  47.4 us
    pallas_call x1, Pallas kernels, fused(): pl.pallas_call(finish_kernel, name='finish', grid=(couples,), out_shape=(...  8.66 us

profile of v3, /device:TPU:0, one launch (start us, length us, event | category | flops | bytes accessed | tf_op | source)
XLA Modules:
  0.0 58.2 jit_solution(11418206106105524627)
XLA Ops:
  0.6 0.7 %constant_dynamic-slice_fusion = (s32[1,4,64,1]{2,3,1,0:T(1,128)S(1)}, s32[1,4,64,1]{2,3,1,0:T(1,128)S(1)}) fusion(s32[1,8,64,1]{2,3,1,0:T(1,128)} %param.13, s32[]{:T(128)S(6)} %select_n.4, s32[1,8,64,1]{2,3,1,0:T(1,128)} %param.12), kind=kLoop, calls=%fused_computation.1 | loop fusion | bytes 4100 | tf_op jit(solution)/shard_map/dynamic_slice | solution.py:555
  1.4 0.1 copy.15
  1.4 0.6 %pad.4.routes_in = s32[64,128]{1,0:T(8,128)} pad(s32[64,8]{1,0:T(8,128)S(1)} %bitcast.12, s32[]{:T(128)} %constant.4.clone.1), padding=0_0x0_120 | pad | bytes 34820 | tf_op jit(solution)/shard_map/jit(_pad)/pad | solution.py:559
  2.1 47.4 %fused.1 = (bf16[8,4096]{1,0:T(8,128)(2,1)}, bf16[2,4,32,128]{3,2,1,0:T(8,128)(2,1)}, bf16[2,4,32,128]{3,2,1,0:T(8,128)(2,1)}, bf16[2,1024,256]{2,1,0:T(8,128)(2,1)}, bf16[2,8,256,256]{3,2,1,0:T(8,128)(2,1)}) custom-call(bf16[8,4096]{1,0:T(8,128)(2,1)} %bitcast.13, bf16[8,4096]{1,0:T(8,128)(2,1)} %bitcast.14, bf16[32,8,128]{2,1,0:T(8,128)(2,1)} %bitcast.15, ...), custom_call_target="tpu_custom_call" | custom-call | tf_op jit(solution)/shard_map/fused/pallas_call | solution.py:567
  49.5 8.7 %finish.1 = (bf16[8,4096]{1,0:T(8,128)(2,1)}, bf16[32,8,128]{2,1,0:T(8,128)(2,1)}, bf16[32,8,128]{2,1,0:T(8,128)(2,1)}, bf16[16,1024,128]{2,1,0:T(8,128)(2,1)}, bf16[16,1024,128]{2,1,0:T(8,128)(2,1)}) custom-call(bf16[2,1024,256]{2,1,0:T(8,128)(2,1)} %get-tuple-element.15.flat_t, bf16[2,8,256,256]{3,2,1,0:T(8,128)(2,1)} %get-tuple-element.16.masked, ...), custom_call_target="tpu_custom_call" | custom-call | tf_op jit(solution)/shard_map/finish/pallas_call | solution.py:633
  (1 shorter events, 0.0 us)
